TPU v7x, 128 devices: a whole 4x4x4 slice. The times are simulated.
128 devices in a mesh: dp: 4 (over y), graph: 32 (over z, x, core).
Axes of the slice: x: 4, y: 4, z: 4, core: 2. Of those that a mesh axis runs over, the one named last changes fastest.
Arguments:
- edge_emb: bfloat16 [4, 16384, 512], P('dp', 'graph'), may hold values from -6 to 6
- atom_emb: bfloat16 [4, 1024, 512], P('dp', 'graph'), may hold values from -6 to 6
- edge_target: int32 [4, 16384], P('dp', 'graph'), may hold values from 0 to 1023, as said below
- trip_in: int32 [4, 524288], P('dp', 'graph'), may hold values from 0 to 16383, as said below
- trip_out: int32 [4, 524288], P('dp', 'graph'), may hold values from 0 to 511
- trip_count: int32 [4, 32], P('dp', 'graph'), may hold values from 8192 to 16384, as said below
- trip_basis: bfloat16 [4, 16, 524288], P('dp', None, 'graph'), may hold values from -3 to 3
- grad_edge: bfloat16 [4, 16384, 512], P('dp', 'graph'), may hold values from -6 to 6
- grad_atom: bfloat16 [4, 1024, 512], P('dp', 'graph'), may hold values from -6 to 6
- w_down: bfloat16 [512, 64], replicated, may hold values from -0.25 to 0.25
- w_bil: bfloat16 [1024, 64], replicated, may hold values from -0.1875 to 0.1875
- w_up: bfloat16 [64, 512], replicated, may hold values from -0.75 to 0.75
- w_atom: bfloat16 [512, 512], replicated, may hold values from -0.25 to 0.25
Outputs:
- edge_new: bfloat16 [4, 16384, 512], P('dp', 'graph')
- atom_new: bfloat16 [4, 1024, 512], P('dp', 'graph')
- grad_edge_in: float32 [4, 16384, 512], P('dp', 'graph')
- grad_wdown: float32 [512, 64], replicated
- grad_wbil: float32 [1024, 64], replicated
- grad_wup: float32 [64, 512], replicated
- grad_watom: float32 [512, 512], replicated
Inputs may be any that keep to these rules, and one draw needn't show every extreme that they name: `trip_in`: among the 16384 slots of one device, the incoming edges held by any one device of the batch number at most 128 distinct ones; on every device some one device gives exactly 128. `trip_count`: every batch has a device with all 16384 slots used. `edge_target`: among the 512 edges of one device, those whose target atom is held by any one device (target // 32) number at most 32; on every device some one holder gets exactly 32.
All inputs are finite; a program needn't handle non-finite values.
Results may differ from a plain program's by a relative error of at most 0.0077.
Values may be sent and summed in bfloat16 or wider, within the bound.
A program may use at most 64 MiB of HBM per device.

v0:
```python
import math

import jax
import jax.numpy as jnp
from jax import lax
from jax.sharding import Mesh
from jax.sharding import PartitionSpec as P

GRAPH = ("graph_0", "graph_1", "graph_2")


ATOM_SCALE = 0.25
BLOCK_LIMIT = 2048


def from_everyone(value, axis):
    copies = jnp.broadcast_to(value, (lax.axis_size(axis), *value.shape))
    return lax.all_to_all(copies, axis, split_axis=0, concat_axis=0, tiled=True)


def laid_out(blocks, dim):
    shape = list(blocks.shape[1:])
    shape[dim] *= blocks.shape[0]
    return jnp.moveaxis(blocks, 0, dim).reshape(shape)


def whole_of(value, axes, dim):
    far, near = axes
    blocks = from_everyone(from_everyone(value, far), near)
    return laid_out(blocks.swapaxes(0, 1).reshape(-1, *value.shape), dim)


def in_blocks(value, dim, peers):
    shape = value.shape
    blocks = value.reshape(*shape[:dim], peers, shape[dim] // peers, *shape[dim + 1 :])
    return jnp.moveaxis(blocks, dim, 0)


def sent_and_summed(value, axis, dim):
    peers = lax.axis_size(axis)
    blocks = lax.all_to_all(in_blocks(value, dim, peers), axis, 0, 0, tiled=True)
    return jnp.sum(blocks, axis=0)


def gather_directly(value, axis, dim):
    return laid_out(from_everyone(value, axis), dim)


def sum_in_two_steps(value, axes, dim):
    far, near = axes
    blocks = in_blocks(value, dim, lax.axis_size(far))
    nearer = sent_and_summed(blocks, near, dim + 1)
    arrived = lax.all_to_all(nearer, far, split_axis=0, concat_axis=0, tiled=True)
    return arrived.sum(axis=0)


def filled_up(lines, peers):
    spare = -len(lines) % peers
    return jnp.pad(lines, [(0, spare)] + [(0, 0)] * (lines.ndim - 1))


def sum_by_parts(value, axes):
    padded = filled_up(value, lax.axis_size(axes[0]) * lax.axis_size(axes[1]))
    whole = whole_of(sum_in_two_steps(padded, axes, 0), axes, 0)
    return lax.slice_in_dim(whole, 0, len(value)).reshape(value.shape)


def in_one(arrays, axis):
    ends = [0]
    for a in arrays:
        ends.append(ends[-1] + a.size)
    total = sum_by_parts(jnp.concatenate([a.ravel() for a in arrays]), axis)
    return tuple((total[b:e].reshape(a.shape) for a, b, e in zip(arrays, ends, ends[1:])))


def silu_slope(value):
    logistic = jax.nn.sigmoid(value)
    return logistic * (1.0 + value * (1.0 - logistic))


def spread_cols(basis_part, feat_part):
    outer = basis_part.astype(jnp.float32)[:, None, :] * feat_part.astype(jnp.float32)[None, :, :]
    return outer.reshape(-1, basis_part.shape[1]).astype(jnp.bfloat16)


def body(
    edge_emb,
    atom_emb,
    edge_target,
    trip_in,
    trip_out,
    trip_count,
    trip_basis,
    grad_edge,
    grad_atom,
    w_down,
    w_bil,
    w_up,
    w_atom,
):
    members = lax.axis_size(GRAPH)
    edge_rows = edge_emb[0]
    edge_dev = edge_rows.shape[0]
    atom_dev = atom_emb.shape[1]
    trip_dev = trip_in.shape[1]
    width_trip = w_down.shape[1]
    basis_width = trip_basis.shape[1]
    block_rows = math.gcd(trip_dev, BLOCK_LIMIT)
    block_count = trip_dev // block_rows
    incoming = trip_in[0]
    outgoing = trip_out[0]
    basis_cols = trip_basis[0]
    targets = edge_target[0]
    edge_iota = jnp.arange(edge_dev, dtype=jnp.int32)
    usable = (jnp.arange(trip_dev, dtype=jnp.int32) < trip_count[0, 0]).astype(jnp.float32)
    contract_first = (((0,), (0,)), ((), ()))
    contract_last = (((1,), (1,)), ((), ()))
    projected = jnp.dot(edge_rows, w_down, preferred_element_type=jnp.float32)
    edge_feat = jax.nn.silu(projected).astype(jnp.bfloat16)
    edge_table_all = whole_of(edge_feat, (("graph_0", "graph_1"), "graph_2"), 0)
    feat_in = jnp.take(edge_table_all, incoming, axis=0).T

    def forward_step(step_index, running):
        offset_at = step_index * block_rows
        feat_part = lax.dynamic_slice_in_dim(feat_in, offset_at, block_rows, 1)
        basis_part = lax.dynamic_slice_in_dim(basis_cols, offset_at, block_rows, 1)
        usable_part = lax.dynamic_slice_in_dim(usable, offset_at, block_rows, 0)
        target_part = lax.dynamic_slice_in_dim(outgoing, offset_at, block_rows, 0)
        spread = spread_cols(basis_part, feat_part)
        mixed = (
            lax.dot_general(w_bil, spread, contract_first, preferred_element_type=jnp.float32)
            * usable_part[None, :]
        )
        one_hot = (target_part[:, None] == edge_iota[None, :]).astype(jnp.float32)
        return running + jnp.dot(
            mixed, one_hot, precision=lax.Precision.HIGHEST, preferred_element_type=jnp.float32
        )

    gathered = lax.fori_loop(
        0, block_count, forward_step, jnp.zeros((width_trip, edge_dev), jnp.float32)
    ).astype(jnp.bfloat16)
    update = lax.dot_general(gathered, w_up, contract_first, preferred_element_type=jnp.float32)
    edge_new = (edge_rows.astype(jnp.float32) + jax.nn.silu(update)).astype(jnp.bfloat16)
    atoms_all = atom_dev * members
    atom_hot_all = (jnp.arange(atoms_all, dtype=jnp.int32)[:, None] == targets[None, :]).astype(
        jnp.bfloat16
    )
    partial_value = jnp.dot(atom_hot_all, edge_new, preferred_element_type=jnp.float32)
    atom_sum = sent_and_summed(partial_value, GRAPH, 0).astype(jnp.bfloat16)
    atom_pre = ATOM_SCALE * jnp.dot(atom_sum, w_atom, preferred_element_type=jnp.float32)
    atom_new = (atom_emb[0].astype(jnp.float32) + jax.nn.silu(atom_pre)).astype(jnp.bfloat16)
    grad_pre = (grad_atom[0].astype(jnp.float32) * silu_slope(atom_pre)).astype(jnp.bfloat16)
    watom_term = ATOM_SCALE * lax.dot_general(
        atom_sum, grad_pre, contract_first, preferred_element_type=jnp.float32
    )
    grad_sum = (
        ATOM_SCALE
        * lax.dot_general(grad_pre, w_atom, contract_last, preferred_element_type=jnp.float32)
    ).astype(jnp.bfloat16)
    grad_all = gather_directly(grad_sum, GRAPH, 0)
    target_grad = jnp.take(grad_all, targets, axis=0)
    grad_new = grad_edge[0].astype(jnp.float32) + target_grad.astype(jnp.float32)
    grad_update = (grad_new * silu_slope(update)).astype(jnp.bfloat16)
    wup_term = jnp.dot(gathered, grad_update, preferred_element_type=jnp.float32)
    grad_gathered = lax.dot_general(
        w_up, grad_update, contract_last, preferred_element_type=jnp.float32
    ).astype(jnp.bfloat16)

    def backward_step(step_index, carried):
        running, grad_feat = carried
        offset_at = step_index * block_rows
        feat_part = lax.dynamic_slice_in_dim(feat_in, offset_at, block_rows, 1)
        basis_part = lax.dynamic_slice_in_dim(basis_cols, offset_at, block_rows, 1)
        usable_part = lax.dynamic_slice_in_dim(usable, offset_at, block_rows, 0)
        target_part = lax.dynamic_slice_in_dim(outgoing, offset_at, block_rows, 0)
        pick_hot = (edge_iota[:, None] == target_part[None, :]).astype(jnp.bfloat16)
        grad_part = jnp.dot(grad_gathered, pick_hot, preferred_element_type=jnp.float32).astype(
            jnp.bfloat16
        )
        grad_part = grad_part * usable_part.astype(jnp.bfloat16)[None, :]
        spread = spread_cols(basis_part, feat_part)
        running = running + lax.dot_general(
            spread, grad_part, contract_last, preferred_element_type=jnp.float32
        )
        backed = jnp.dot(w_bil, grad_part, preferred_element_type=jnp.float32).reshape(
            basis_width, width_trip, block_rows
        )
        feat_grad = jnp.sum(basis_part.astype(jnp.float32)[:, None, :] * backed, axis=0)
        return (running, lax.dynamic_update_slice_in_dim(grad_feat, feat_grad, offset_at, 1))

    wbil_term, grad_feat = lax.fori_loop(
        0,
        block_count,
        backward_step,
        (jnp.zeros(w_bil.shape, jnp.float32), jnp.zeros((width_trip, trip_dev), jnp.float32)),
    )
    grad_feat_rows = grad_feat.T
    spread_back = jax.ops.segment_sum(grad_feat_rows, incoming, num_segments=members * edge_dev)
    grad_edge_feat = sum_in_two_steps(spread_back, (("graph_0", "graph_1"), "graph_2"), 0)
    grad_project = (grad_edge_feat * silu_slope(projected)).astype(jnp.bfloat16)
    grad_edge_in = grad_new + lax.dot_general(
        grad_project, w_down, contract_last, preferred_element_type=jnp.float32
    )
    wdown_term = lax.dot_general(
        edge_rows, grad_project, contract_first, preferred_element_type=jnp.float32
    )
    totals = in_one(
        (wdown_term, wbil_term, wup_term, watom_term), (("dp", "graph_0", "graph_1"), "graph_2")
    )
    factor = 1.0 / math.sqrt(lax.axis_size("dp") * members * edge_dev)
    return (
        edge_new[None],
        atom_new[None],
        grad_edge_in[None],
        totals[0] * factor,
        totals[1] * factor,
        totals[2] * factor,
        totals[3] * factor,
    )


def solution(mesh):
    finer = Mesh(
        mesh.devices.reshape(mesh.shape["dp"], 4, 4, 2), ("dp", "graph_0", "graph_1", "graph_2")
    )
    placed = (
        P("dp", GRAPH, None),
        P("dp", GRAPH, None),
        P("dp", GRAPH),
        P("dp", GRAPH),
        P("dp", GRAPH),
        P("dp", GRAPH),
        P("dp", None, GRAPH),
        P("dp", GRAPH, None),
        P("dp", GRAPH, None),
        P(),
        P(),
        P(),
        P(),
    )
    return jax.shard_map(
        body,
        mesh=finer,
        in_specs=placed,
        out_specs=(
            P("dp", GRAPH, None),
            P("dp", GRAPH, None),
            P("dp", GRAPH, None),
            P(),
            P(),
            P(),
            P(),
        ),
        check_vma=False,
    )
```

profile of v0, /device:TPU:1, one launch (start us, length us, event | category | flops | bytes accessed | tf_op | source)
XLA Modules:
  0.0 566.6 jit_solution(12635531151740514370)
XLA Ops:
  3.2 8.4 %all-to-all-start = ((bf16[16,512,64]{1,2,0:T(8,128)(2,1)}), bf16[16,512,64]{1,2,0:T(8,128)(2,1)S(1)}, u32[]{:S(2)}, u32[]{:S(2)}) async-start(bf16[16,512,64]{1,2,0:T(8,128)(2,1)} %broadcast_in_dim.90), calls=%async_computation | async-start | bytes 2097152 | tf_op jit(solution)/shard_map/all_to_all | solution.py:18
  12.4 15.2 %all-to-all-done = bf16[16,512,64]{1,2,0:T(8,128)(2,1)S(1)} async-done(((bf16[16,512,64]{1,2,0:T(8,128)(2,1)}), bf16[16,512,64]{1,2,0:T(8,128)(2,1)S(1)}, u32[]{:S(2)}, u32[]{:S(2)}) %all-to-all-start) | async-done | bytes 1048608 | tf_op jit(solution)/shard_map/all_to_all | solution.py:18
  27.9 7.6 %all_to_all.58 = bf16[2,16,512,64]{2,3,1,0:T(8,128)(2,1)S(1)} all-to-all(bf16[2,16,512,64]{2,3,1,0:T(8,128)(2,1)S(1)} %broadcast_in_dim.91), channel_id=1, replica_groups=mesh['dp'=4,'graph_0'=4,'graph_1'=4,'graph_2'=2] {'graph_2'}, dimensions={0} | all-to-all | bytes 4194304 | tf_op jit(solution)/shard_map/all_to_all | solution.py:18
  38.7 58.1 %gather_fusion = bf16[16384,64]{1,0:T(8,128)(2,1)} fusion(bf16[16384,64]{1,0:T(8,128)(2,1)} %bitcast.114, s32[16384]{0:T(1024)S(1)} %broadcast_clamp_fusion), kind=kCustom, calls=%fused_computation | custom fusion | bytes 4259840 | tf_op jit(solution)/shard_map/jit(_take)/gather | solution.py:121
  96.8 11.5 %select_bitcast_fusion = bf16[64,16384]{0,1:T(8,128)(2,1)} fusion(bf16[16384,64]{1,0:T(8,128)(2,1)} %gather_fusion, pred[16384]{0:T(1024)(128)(4,1)S(1)} %compare_and_fusion), kind=kLoop, calls=%fused_computation.27 | loop fusion | flops 1048576 | bytes 4210688 | tf_op jit(solution)/shard_map/jit(_take)/select_n | solution.py:121
  108.4 4.8 copy.43
  113.2 49.3 %while.30 = (s32[]{:T(128)}, f32[64,512]{1,0:T(8,128)S(1)}, bf16[16,16384]{1,0:T(8,128)(2,1)}, bf16[64,16384]{1,0:T(8,128)(2,1)}, bf16[1024,64]{0,1:T(8,128)(2,1...) while((s32[]{:T(128)}, f32[64,512]{1,0:T(8,128)S(1)}, ...), condition=%wide.region_1.2_spmd.clone, body=%wide.region_0.1_spmd.clone.sunk | while | flops 1079345152 | bytes 11518133 | solution.py:139
  164.6 32.1 %all_to_all.59 = f32[32,32,512]{2,1,0:T(8,128)} all-to-all(f32[32,32,512]{2,1,0:T(8,128)S(1)} %bitcast.124), channel_id=1, replica_groups=mesh['dp'=4,'graph_0'=4,'graph_1'=4,'graph_2'=2] {'graph_0','graph_1','g..., dimensions={0} | all-to-all | bytes 4194304 | tf_op jit(solution)/shard_map/all_to_all | solution.py:41
  200.1 4.0 all-to-all-start.3
  204.1 17.1 %all-to-all-done.3 = bf16[32,32,512]{2,1,0:T(8,128)(2,1)S(1)} async-done(((bf16[32,32,512]{2,1,0:T(8,128)(2,1)}), bf16[32,32,512]{2,1,0:T(8,128)(2,1)S(1)}, u32[]{:S(2)}, u32[]{:S(2)}) %all-to-all-start.3) | async-done | bytes 1048608 | tf_op jit(solution)/shard_map/all_to_all | solution.py:18
  227.7 100.8 %while.31 = (s32[]{:T(128)}, f32[1024,64]{0,1:T(8,128)S(1)}, f32[64,16384]{1,0:T(8,128)}, bf16[16,16384]{1,0:T(8,128)(2,1)}, bf16[64,16384]{1,0:T(8,128)(2,1)}, ...) while((s32[]{:T(128)}, f32[1024,64]{0,1:T(8,128)S(1)}, ...), condition=%wide.region_5.6_spmd.clone, body=%wide.region_3.5_spmd.clone.sunk | while | flops 680951808 | bytes 29921480 | solution.py:191
  232.4 3.4 multiply_reduce_fusion.2
  236.6 3.6 convolution_add_fusion.3
  249.2 3.6 convolution_add_fusion.3
  261.8 3.6 convolution_add_fusion.3
  274.4 3.6 convolution_add_fusion.3
  287.1 3.6 convolution_add_fusion.3
  299.7 3.6 convolution_add_fusion.3
  312.3 3.6 convolution_add_fusion.3
  324.9 3.6 convolution_add_fusion.3
  328.5 6.9 %copy.45 = f32[16384,64]{1,0:T(8,128)} copy(f32[16384,64]{0,1:T(8,128)} %bitcast.117) | data formatting | bytes 8388608 | tf_op jit(solution)/shard_map/transpose | solution.py:197
  335.4 91.3 %scatter_custom_fusion = f32[16384,64]{1,0:T(8,128)} fusion(s32[16384]{0:T(1024)S(1)} %bitcast.128, f32[16384,64]{1,0:T(8,128)} %copy.45, f32[]{:T(128)} %constant.108.clone.1), kind=kCustom, calls=%fused_computation.25 | custom fusion | flops 1048576 | bytes 4194816 | tf_op jit(solution)/shard_map/scatter-add | solution.py:198
  426.8 6.8 %copy.46 = f32[16,2,512,64]{2,3,0,1:T(8,128)} copy(f32[16,2,512,64]{3,2,1,0:T(8,128)} %bitcast.115) | data formatting | bytes 8388608 | tf_op jit(solution)/shard_map/reshape;reshape | solution.py:35
  433.6 11.9 %all_to_all.60 = f32[2,16,512,64]{2,3,1,0:T(8,128)} all-to-all(f32[2,16,512,64]{2,3,1,0:T(8,128)} %bitcast.118), channel_id=1, replica_groups=mesh['dp'=4,'graph_0'=4,'graph_1'=4,'graph_2'=2] {'graph_2'}, dimensions={0} | all-to-all | bytes 8388608 | tf_op jit(solution)/shard_map/all_to_all | solution.py:41
  445.4 4.2 reduce_sum.59
  449.6 4.1 all-to-all-start.5
  458.8 27.7 %all-to-all-done.5 = f32[16,512,64]{1,2,0:T(8,128)S(1)} async-done(((f32[16,512,64]{1,2,0:T(8,128)}), f32[16,512,64]{1,2,0:T(8,128)S(1)}, u32[]{:S(2)}, u32[]{:S(2)}) %all-to-all-start.5) | async-done | bytes 2097184 | tf_op jit(solution)/shard_map/all_to_all | solution.py:53
  493.4 5.9 %all_to_all.61 = f32[2,64,3072]{2,1,0:T(8,128)S(1)} all-to-all(f32[2,64,3072]{2,1,0:T(8,128)S(1)} %copy.49), channel_id=1, replica_groups=mesh['dp'=4,'graph_0'=4,'graph_1'=4,'graph_2'=2] {'graph_2'}, dimensions={0} | all-to-all | bytes 3145728 | tf_op jit(solution)/shard_map/all_to_all | solution.py:41
  502.0 22.0 %all_to_all.62 = f32[64,1,3072]{2,1,0:T(1,128)S(1)} all-to-all(f32[64,1,3072]{2,1,0:T(1,128)S(1)} %all_to_all.43), channel_id=1, replica_groups=mesh['dp'=4,'graph_0'=4,'graph_1'=4,'graph_2'=2] {'dp','graph_0','graph_1'}, dimensions={0} | all-to-all | bytes 1572864 | tf_op jit(solution)/shard_map/all_to_all | solution.py:53
  525.7 4.6 all-to-all-start.8
  532.3 12.2 %all-to-all-done.8 = f32[64,1,3072]{2,1,0:T(1,128)S(1)} async-done(((f32[64,1,3072]{2,1,0:T(1,128)}), f32[64,1,3072]{2,1,0:T(1,128)S(1)}, u32[]{:S(2)}, u32[]{:S(2)}) %all-to-all-start.8) | async-done | bytes 786464 | tf_op jit(solution)/shard_map/all_to_all | solution.py:18
  544.9 7.6 %all_to_all.63 = f32[2,64,3072]{2,1,0:T(8,128)S(1)} all-to-all(f32[2,64,3072]{2,1,0:T(8,128)S(1)} %broadcast_in_dim.103), channel_id=1, replica_groups=mesh['dp'=4,'graph_0'=4,'graph_1'=4,'graph_2'=2] {'graph_2'}, dimensions={0} | all-to-all | bytes 3145728 | tf_op jit(solution)/shard_map/all_to_all | solution.py:18
  (203 shorter events, 167.6 us)
Async XLA Ops:
  0.6 197.9 %copy-start = (bf16[512,512]{1,0:T(8,128)(2,1)S(1)}, bf16[512,512]{1,0:T(8,128)(2,1)}, u32[]{:S(2)}) copy-start(bf16[512,512]{1,0:T(8,128)(2,1)} %param.29) | copy-start | bytes 1572868
  0.6 10.9 %copy-start.6 = (s32[1,16384]{1,0:T(1,128)S(1)}, s32[1,16384]{1,0:T(1,128)}, u32[]{:S(2)}) copy-start(s32[1,16384]{1,0:T(1,128)} %param.20) | copy-start | bytes 196612
  3.2 24.5 %all-to-all-start = ((bf16[16,512,64]{1,2,0:T(8,128)(2,1)}), bf16[16,512,64]{1,2,0:T(8,128)(2,1)S(1)}, u32[]{:S(2)}, u32[]{:S(2)}) async-start(bf16[16,512,64]{1,2,0:T(8,128)(2,1)} %broadcast_in_dim.90), calls=%async_computation | async-start | bytes 2097152 | tf_op jit(solution)/shard_map/all_to_all | solution.py:18
  108.4 4.8 copy-start.2
  113.2 49.3 %copy-start.5 = (bf16[1,512,512]{2,1,0:T(8,128)(2,1)S(1)}, bf16[1,512,512]{2,1,0:T(8,128)(2,1)}, u32[]{:S(2)}) copy-start(bf16[1,512,512]{2,1,0:T(8,128)(2,1)} %param.17) | copy-start | bytes 1572868
  113.2 49.4 %copy-start.9 = (bf16[64,512]{1,0:T(8,128)(2,1)S(1)}, bf16[64,512]{1,0:T(8,128)(2,1)}, u32[]{:S(2)}) copy-start(bf16[64,512]{1,0:T(8,128)(2,1)} %param.28) | copy-start | bytes 196612
  162.5 34.3 %copy-start.7 = (f32[64,512]{1,0:T(8,128)}, f32[64,512]{1,0:T(8,128)S(1)}, u32[]{:S(2)}) copy-start(f32[64,512]{1,0:T(8,128)S(1)} %get-tuple-element.316) | copy-start | bytes 393220
  162.5 1.4 copy-start.13
  163.9 34.6 %copy-start.14 = (bf16[512,512]{1,0:T(8,128)(2,1)}, bf16[512,512]{1,0:T(8,128)(2,1)S(1)}, u32[]{:S(2)}) copy-start(bf16[512,512]{1,0:T(8,128)(2,1)S(1)} %get-tuple-element.500) | copy-start | bytes 1572868
  164.6 34.1 %copy-start.11 = (bf16[1,32,512]{2,1,0:T(8,128)(2,1)S(1)}, bf16[1,32,512]{2,1,0:T(8,128)(2,1)}, u32[]{:S(2)}) copy-start(bf16[1,32,512]{2,1,0:T(8,128)(2,1)} %param.25) | copy-start | bytes 98308
  200.1 21.2 %all-to-all-start.3 = ((bf16[32,32,512]{2,1,0:T(8,128)(2,1)}), bf16[32,32,512]{2,1,0:T(8,128)(2,1)S(1)}, u32[]{:S(2)}, u32[]{:S(2)}) async-start(bf16[32,32,512]{2,1,0:T(8,128)(2,1)} %broadcast_in_dim.96), calls=%async_computation.3 | async-start | bytes 2097152 | tf_op jit(solution)/shard_map/all_to_all | solution.py:18
  225.1 2.6 copy-start.3
  449.6 5.6 copy-start.8
  449.6 36.8 %all-to-all-start.5 = ((f32[16,512,64]{1,2,0:T(8,128)}), f32[16,512,64]{1,2,0:T(8,128)S(1)}, u32[]{:S(2)}, u32[]{:S(2)}) async-start(f32[16,512,64]{1,2,0:T(8,128)} %reduce_sum.59), calls=%async_computation.5 | async-start | bytes 4194304 | tf_op jit(solution)/shard_map/all_to_all | solution.py:53
  499.3 31.1 %copy-start.12 = (bf16[1,32,512]{2,1,0:T(8,128)(2,1)S(1)}, bf16[1,32,512]{2,1,0:T(8,128)(2,1)}, u32[]{:S(2)}) copy-start(bf16[1,32,512]{2,1,0:T(8,128)(2,1)} %param.18) | copy-start | bytes 98308
  499.3 31.8 %copy-start.4 = (bf16[1,512,512]{2,1,0:T(8,128)(2,1)S(1)}, bf16[1,512,512]{2,1,0:T(8,128)(2,1)}, u32[]{:S(2)}) copy-start(bf16[1,512,512]{2,1,0:T(8,128)(2,1)} %param.24) | copy-start | bytes 1572868
  499.3 31.8 %copy-start.10 = (bf16[512,64]{0,1:T(8,128)(2,1)S(1)}, bf16[512,64]{0,1:T(8,128)(2,1)}, u32[]{:S(2)}) copy-start(bf16[512,64]{0,1:T(8,128)(2,1)} %param.26) | copy-start | bytes 196612
  525.7 18.8 %all-to-all-start.8 = ((f32[64,1,3072]{2,1,0:T(1,128)}), f32[64,1,3072]{2,1,0:T(1,128)S(1)}, u32[]{:S(2)}, u32[]{:S(2)}) async-start(f32[64,1,3072]{2,1,0:T(1,128)} %broadcast_in_dim.102), calls=%async_computation.8 | async-start | bytes 1572864 | tf_op jit(solution)/shard_map/all_to_all | solution.py:18
  553.7 12.9 %copy-start.1 = (bf16[512,512]{1,0:T(8,128)(2,1)S(1)}, bf16[512,512]{1,0:T(8,128)(2,1)}, u32[]{:S(2)}) copy-start(bf16[512,512]{1,0:T(8,128)(2,1)} %param.29) | copy-start | bytes 1572868
where the time goes:
time: 571 us; the launch traced here: 567 us
  other arithmetic  185 us (32%)
  local copies, waits for them, and re-layouts  124 us (22%)
  blocking collectives  87 us (15%)
  matrix products  74.9 us (13%)
  waiting for transfers between devices  72.3 us (13%)
  starting transfers between devices  21.1 us (4%)
    scatter-add x1, other arithmetic, body(): jax.ops.segment_sum(grad_feat_rows, incoming, num_segments=members * edge...  91.3 us
    gather x1, local copies, waits for them, and re-layouts, body(): feat_in = jnp.take(edge_table_all, incoming, axis=0).T  58.1 us
    all_to_all x3, blocking collectives, sent_and_summed(): lax.all_to_all(in_blocks(value, dim, peers), axis, 0, 0, tiled=True)  49.8 us
    all_to_all x3, waiting for transfers between devices, from_everyone(): return lax.all_to_all(copies, axis, split_axis=0, concat_axis=0, tiled=True)  44.6 us
    dot_general x8, matrix products, backward_step(): lax.dot_general(spread, grad_part, contract_last, preferred_element_type=...  28.9 us
    all_to_all x1, waiting for transfers between devices, sum_in_two_steps(): lax.all_to_all(nearer, far, split_axis=0, concat_axis=0, tiled=True)  27.7 us
    reduce_sum x8, other arithmetic, backward_step(): jnp.sum(basis_part.astype(jnp.float32)[:, None, :] * backed, axis=0)  27.2 us
    all_to_all x1, blocking collectives, sum_in_two_steps(): lax.all_to_all(nearer, far, split_axis=0, concat_axis=0, tiled=True)  22 us
  transfers between devices with their start and end apart: 4, of which 4 were waited for; matrix products, arithmetic and copies ran while one was open for 1% of the time, Pallas kernels for 0%

commit v1 on v0

v1 whole, which is shorter than its diff:
```python
import functools
import math

import jax
import jax.numpy as jnp
from jax import lax
from jax.experimental import pallas as pl
from jax.experimental.pallas import tpu as pltpu
from jax.sharding import PartitionSpec as P

MESH = pl.DeviceIdType.MESH
F32 = jnp.float32
BF16 = jnp.bfloat16
ATOM_SCALE = 0.25
CAP = 128
LANES = 128
NEAR = 4
BLOCK = 1024
ANY = pl.BlockSpec(memory_space=pl.ANY)
VMEM = pl.BlockSpec(memory_space=pltpu.VMEM)
NN = (((1,), (0,)), ((), ()))
NT = (((1,), (1,)), ((), ()))
TN = (((0,), (0,)), ((), ()))


def dot(a, b, dims=NN):
    return lax.dot_general(a, b, dims, preferred_element_type=F32)


def two_part_dot(a, b, dims=NN):
    high = a.astype(BF16)
    low = (a - high.astype(F32)).astype(BF16)
    return dot(high, b, dims) + dot(low, b, dims)


def rows_of(shape):
    return lax.broadcasted_iota(jnp.int32, shape, 0)


def hot(index, size):
    return (rows_of((size, index.shape[1])) == index).astype(F32).astype(BF16)


def silu_slope(value):
    logistic = jax.nn.sigmoid(value)
    return logistic * (1.0 + value * (1.0 - logistic))


def silu(value):
    return value * jax.nn.sigmoid(value)


def params(**kw):
    return pltpu.CompilerParams(vmem_limit_bytes=60 * 1024 * 1024, **kw)


def exchange_kernel(peers, source_at, target_at, x_ref, o_ref, send, recv, own):
    me = lax.axis_index("graph")
    barrier = pltpu.get_barrier_semaphore()

    def greet(k, c):
        pl.semaphore_signal(
            barrier, inc=1, device_id={"graph": lax.rem(me + k, peers)}, device_id_type=MESH
        )
        return c

    lax.fori_loop(1, peers, greet, 0)
    mine = pltpu.make_async_copy(source_at(x_ref, me), target_at(o_ref, me), own)
    mine.start()
    pl.semaphore_wait(barrier, peers - 1)

    def copy(k):
        peer = lax.rem(me + k, peers)
        return pltpu.make_async_remote_copy(
            src_ref=source_at(x_ref, peer),
            dst_ref=target_at(o_ref, me),
            send_sem=send.at[k],
            recv_sem=recv.at[k],
            device_id={"graph": peer},
            device_id_type=MESH,
        )

    def start(k, c):
        copy(k).start()
        return c

    def finish(k, c):
        copy(k).wait()
        return c

    lax.fori_loop(1, peers, start, 0)
    mine.wait()
    lax.fori_loop(1, peers, finish, 0)


def exchange(value, out_shape, source_at, target_at, peers, key):
    return pl.pallas_call(
        functools.partial(exchange_kernel, peers, source_at, target_at),
        out_shape=jax.ShapeDtypeStruct(out_shape, value.dtype),
        in_specs=[ANY],
        out_specs=ANY,
        scratch_shapes=[
            pltpu.SemaphoreType.DMA((peers,)),
            pltpu.SemaphoreType.DMA((peers,)),
            pltpu.SemaphoreType.DMA,
        ],
        compiler_params=params(collective_id=key, has_side_effects=True),
        name=f"exchange_{key}",
    )(value)


def whole_block(ref, index):
    return ref


def lead_block(ref, index):
    return ref.at[index]


def tile_block(ref, index):
    width = ref.shape[1] // NEAR
    rows = 64
    return ref.at[
        pl.ds(pl.multiple_of(lax.div(index, NEAR) * rows, rows), rows),
        pl.ds(pl.multiple_of(lax.rem(index, NEAR) * width, width), width),
    ]


def lane_block(ref, index):
    return ref.at[:, pl.ds(pl.multiple_of(index * CAP, CAP), CAP)]


def row_block(rows, ref, index):
    return ref.at[pl.ds(pl.multiple_of(index * rows, rows), rows), :]


def names_kernel(blocks, members, in_ref, emb_ref, wdt_ref, rank_ref, slot_ref, proj_ref, feat_ref, table, found):
    step = pl.program_id(0)
    highs = table.shape[0]
    per = highs // members
    index = in_ref[...]
    high = lax.shift_right_logical(index, 7)
    low = lax.bitwise_and(index, LANES - 1)

    @pl.when(step == 0)
    def _():
        found[...] = jnp.zeros_like(found)
        proj = dot(wdt_ref[...], emb_ref[...], NT)
        proj_ref[...] = proj
        feat_ref[...] = silu(proj).astype(BF16)

    @pl.when(step < blocks)
    def _():
        found[...] += dot(hot(high, highs), hot(low, LANES), NT)

    @pl.when(step == blocks - 1)
    def _():
        there = jnp.where(found[...] > 0.0, 1.0, 0.0)
        there16 = there.astype(BF16)
        row = lax.broadcasted_iota(jnp.int32, (LANES, LANES), 0)
        col = lax.broadcasted_iota(jnp.int32, (LANES, LANES), 1)
        upper = (row <= col).astype(F32).astype(BF16)
        hrow = lax.broadcasted_iota(jnp.int32, (highs, highs), 0)
        hcol = lax.broadcasted_iota(jnp.int32, (highs, highs), 1)
        before = ((hcol < hrow) & (lax.div(hcol, per) == lax.div(hrow, per))).astype(F32).astype(BF16)
        ahead = dot(before, there16).astype(BF16)
        ones = jnp.ones((LANES, LANES), BF16)
        rank = dot(there16, upper) + dot(ahead, ones) - 1.0
        rank = jnp.where(there > 0.0, rank, -1.0)
        table[...] = rank.astype(BF16)
        for s in range(members):
            rank_ref[s] = rank[s * per : (s + 1) * per, :]

    @pl.when(step >= blocks)
    def _():
        ranks = dot(table[...], hot(high, highs), TN)
        picked = jnp.where(rows_of(ranks.shape) == low, ranks, 0.0)
        rank = jnp.sum(picked, axis=0, keepdims=True).astype(jnp.int32)
        near = lax.bitwise_and(lax.div(high, per), NEAR - 1)
        slot_ref[...] = near * CAP + rank


def names(incoming, emb, wdt, members):
    slots = incoming.shape[1]
    edges = emb.shape[0]
    width = wdt.shape[0]
    block = math.gcd(slots, 2 * BLOCK)
    blocks = slots // block
    highs = members * edges // LANES
    per = highs // members
    return pl.pallas_call(
        functools.partial(names_kernel, blocks, members),
        grid=(2 * blocks,),
        out_shape=(
            jax.ShapeDtypeStruct((members, per, LANES), F32),
            jax.ShapeDtypeStruct((1, slots), jnp.int32),
            jax.ShapeDtypeStruct((width, edges), F32),
            jax.ShapeDtypeStruct((width, edges), BF16),
        ),
        in_specs=[
            pl.BlockSpec((1, block), lambda i: (0, lax.rem(i, blocks))),
            pl.BlockSpec(emb.shape, lambda i: (0, 0)),
            pl.BlockSpec(wdt.shape, lambda i: (0, 0)),
        ],
        out_specs=(
            pl.BlockSpec((members, per, LANES), lambda i: (0, 0, 0)),
            pl.BlockSpec((1, block), lambda i: (0, lax.max(i - blocks, 0))),
            pl.BlockSpec((width, edges), lambda i: (0, 0)),
            pl.BlockSpec((width, edges), lambda i: (0, 0)),
        ),
        scratch_shapes=[pltpu.VMEM((highs, LANES), BF16), pltpu.VMEM((highs, LANES), F32)],
        compiler_params=params(),
        name="names",
    )(incoming, emb, wdt)


def chosen_hot(rank_ref, member):
    per = rank_ref.shape[1]
    ranks = rank_ref[member]
    place = lax.broadcasted_iota(jnp.int32, (CAP, LANES), 0).astype(F32)
    return jnp.concatenate(
        [(place == ranks[q : q + 1, :]).astype(F32).astype(BF16) for q in range(per)], axis=1
    )


def select_kernel(members, rank_ref, feat_ref, out_ref):
    def one(d, c):
        out_ref[d] = dot(feat_ref[...], chosen_hot(rank_ref, d), NT).astype(BF16)
        return c

    lax.fori_loop(0, members, one, 0)


def select(ranks, feat):
    members = ranks.shape[0]
    return pl.pallas_call(
        functools.partial(select_kernel, members),
        out_shape=jax.ShapeDtypeStruct((members, feat.shape[0], CAP), BF16),
        in_specs=[VMEM, VMEM],
        out_specs=VMEM,
        compiler_params=params(),
        name="select",
    )(ranks, feat)


def forward_kernel(
    blocks, edges, far, table_ref, slot_ref, in_ref, out_ref, count_ref, basis_ref, total_ref, spread
):
    step = pl.program_id(0)
    block = slot_ref.shape[1]
    width = table_ref.shape[0] // far
    shift = edges.bit_length() - 1 + NEAR.bit_length() - 1

    @pl.when(step == 0)
    def _():
        total_ref[...] = jnp.zeros_like(total_ref)

    group = lax.shift_right_logical(in_ref[...], shift)
    wide = dot(table_ref[...], hot(slot_ref[...], table_ref.shape[1]))
    feat = wide[0:width]
    for k in range(1, far):
        feat = jnp.where(group == k, wide[k * width : (k + 1) * width], feat)
    basis = basis_ref[...].astype(F32)
    for b in range(basis.shape[0]):
        spread[b * width : (b + 1) * width, :] = (basis[b : b + 1, :] * feat).astype(BF16)
    at = step * block + lax.broadcasted_iota(jnp.int32, (1, block), 1)
    place = jnp.where(at < count_ref[0, 0], out_ref[...], -1)
    total_ref[...] += dot(spread[...], hot(place, edges), NT)


def forward(table, slots, incoming, outgoing, count, basis, edges):
    total = slots.shape[1]
    block = math.gcd(total, BLOCK)
    blocks = total // block
    far = table.shape[0] // 64
    rows = basis.shape[0] * 64
    line = pl.BlockSpec((1, block), lambda i: (0, i))
    return pl.pallas_call(
        functools.partial(forward_kernel, blocks, edges, far),
        grid=(blocks,),
        out_shape=jax.ShapeDtypeStruct((rows, edges), F32),
        in_specs=[
            pl.BlockSpec(table.shape, lambda i: (0, 0)),
            line,
            line,
            line,
            pl.BlockSpec(memory_space=pltpu.SMEM),
            pl.BlockSpec((basis.shape[0], block), lambda i: (0, i)),
        ],
        out_specs=pl.BlockSpec((rows, edges), lambda i: (0, 0)),
        scratch_shapes=[pltpu.VMEM((rows, block), BF16)],
        compiler_params=params(),
        name="forward",
    )(table, slots, incoming, outgoing, count, basis)


def edges_kernel(total_ref, wbt_ref, wup_ref, emb_ref, target_ref, gath_ref, new_ref, slope_ref, atoms_ref):
    total = total_ref[...]
    high = total.astype(BF16)
    low = (total - high.astype(F32)).astype(BF16)
    gathered = (dot(wbt_ref[...], high) + dot(wbt_ref[...], low)).astype(BF16)
    gath_ref[...] = gathered
    update = dot(gathered, wup_ref[...], TN)
    new = (emb_ref[...].astype(F32) + silu(update)).astype(BF16)
    new_ref[...] = new
    slope_ref[...] = silu_slope(update)
    atoms_ref[...] = dot(hot(target_ref[...], atoms_ref.shape[0]), new).astype(BF16)


def edges_forward(total, wbt, wup, emb, targets, atoms):
    edges, wide = emb.shape
    return pl.pallas_call(
        edges_kernel,
        out_shape=(
            jax.ShapeDtypeStruct((wbt.shape[0], edges), BF16),
            jax.ShapeDtypeStruct((edges, wide), BF16),
            jax.ShapeDtypeStruct((edges, wide), F32),
            jax.ShapeDtypeStruct((atoms, wide), BF16),
        ),
        in_specs=[VMEM] * 5,
        out_specs=(VMEM,) * 4,
        compiler_params=params(),
        name="edges",
    )(total, wbt, wup, emb, targets)


def atoms_kernel(part_ref, watom_ref, emb_ref, grad_ref, new_ref, term_ref, sum_ref):
    total = jnp.sum(part_ref[...].astype(F32), axis=0).astype(BF16)
    pre = ATOM_SCALE * dot(total, watom_ref[...])
    new_ref[...] = (emb_ref[...].astype(F32) + silu(pre)).astype(BF16)
    grad_pre = (grad_ref[...].astype(F32) * silu_slope(pre)).astype(BF16)
    term_ref[...] = ATOM_SCALE * dot(total, grad_pre, TN)
    sum_ref[...] = (ATOM_SCALE * dot(grad_pre, watom_ref[...], NT)).astype(BF16)


def atoms_step(parts, watom, emb, grad):
    return pl.pallas_call(
        atoms_kernel,
        out_shape=(
            jax.ShapeDtypeStruct(emb.shape, BF16),
            jax.ShapeDtypeStruct(watom.shape, F32),
            jax.ShapeDtypeStruct(emb.shape, BF16),
        ),
        in_specs=[VMEM] * 4,
        out_specs=(VMEM,) * 3,
        compiler_params=params(),
        name="atoms",
    )(parts, watom, emb, grad)


def turn_kernel(all_ref, target_ref, grad_ref, slope_ref, wup_ref, gath_ref, total_ref, new_ref, up_ref, bil_ref, gg_ref):
    picked = dot(hot(target_ref[...], all_ref.shape[0]), all_ref[...], TN)
    new = grad_ref[...].astype(F32) + picked
    new_ref[...] = new
    update = (new * slope_ref[...]).astype(BF16)
    up_ref[...] = dot(gath_ref[...], update)
    gg = dot(wup_ref[...], update, NT).astype(BF16)
    gg_ref[...] = gg
    total = total_ref[...]
    high = total.astype(BF16)
    low = (total - high.astype(F32)).astype(BF16)
    bil_ref[...] = dot(gg, high, NT) + dot(gg, low, NT)


def turn(grad_all, targets, grad_edge, slope, wup, gathered, total):
    return pl.pallas_call(
        turn_kernel,
        out_shape=(
            jax.ShapeDtypeStruct(grad_edge.shape, F32),
            jax.ShapeDtypeStruct(wup.shape, F32),
            jax.ShapeDtypeStruct((wup.shape[0], total.shape[0]), F32),
            jax.ShapeDtypeStruct(gathered.shape, BF16),
        ),
        in_specs=[VMEM] * 7,
        out_specs=(VMEM,) * 4,
        compiler_params=params(),
        name="turn",
    )(grad_all, targets, grad_edge, slope, wup, gathered, total)


def backward_kernel(
    blocks, edges, far, gg_ref, slot_ref, in_ref, out_ref, count_ref, basis_ref, wbil_ref, sent_ref, total, spread
):
    step = pl.program_id(0)
    block = slot_ref.shape[1]
    width = gg_ref.shape[0]
    shift = edges.bit_length() - 1 + NEAR.bit_length() - 1

    @pl.when(step == 0)
    def _():
        total[...] = jnp.zeros_like(total)

    at = step * block + lax.broadcasted_iota(jnp.int32, (1, block), 1)
    place = jnp.where(at < count_ref[0, 0], out_ref[...], -1)
    picked = dot(gg_ref[...], hot(place, edges)).astype(BF16)
    backed = dot(wbil_ref[...], picked)
    basis = basis_ref[...].astype(F32)
    grad = basis[0:1, :] * backed[0:width]
    for b in range(1, basis.shape[0]):
        grad = grad + basis[b : b + 1, :] * backed[b * width : (b + 1) * width]
    group = lax.shift_right_logical(in_ref[...], shift)
    for k in range(far):
        spread[k * width : (k + 1) * width, :] = jnp.where(group == k, grad, 0.0).astype(BF16)
    total[...] += dot(spread[...], hot(slot_ref[...], total.shape[1]), NT)

    @pl.when(step == blocks - 1)
    def _():
        sent_ref[...] = total[...].astype(BF16)


def backward(gg, slots, incoming, outgoing, count, basis, wbil, far):
    width, edges = gg.shape
    total = slots.shape[1]
    block = math.gcd(total, BLOCK)
    blocks = total // block
    line = pl.BlockSpec((1, block), lambda i: (0, i))
    shape = (far * width, NEAR * CAP)
    return pl.pallas_call(
        functools.partial(backward_kernel, blocks, edges, far),
        grid=(blocks,),
        out_shape=jax.ShapeDtypeStruct(shape, BF16),
        in_specs=[
            pl.BlockSpec(gg.shape, lambda i: (0, 0)),
            line,
            line,
            line,
            pl.BlockSpec(memory_space=pltpu.SMEM),
            pl.BlockSpec((basis.shape[0], block), lambda i: (0, i)),
            pl.BlockSpec(wbil.shape, lambda i: (0, 0)),
        ],
        out_specs=pl.BlockSpec(shape, lambda i: (0, 0)),
        scratch_shapes=[pltpu.VMEM(shape, F32), pltpu.VMEM((far * width, block), BF16)],
        compiler_params=params(),
        name="backward",
    )(gg, slots, incoming, outgoing, count, basis, wbil)


def last_kernel(members, back_ref, rank_ref, proj_ref, wdt_ref, emb_ref, new_ref, in_ref, down_ref):
    def one(d, total):
        block = back_ref[:, pl.ds(pl.multiple_of(d * CAP, CAP), CAP)]
        return total + dot(block, chosen_hot(rank_ref, d))

    grad = lax.fori_loop(0, members, one, jnp.zeros(proj_ref.shape, F32))
    grad = (grad * silu_slope(proj_ref[...])).astype(BF16)
    in_ref[...] = new_ref[...] + dot(grad, wdt_ref[...], TN)
    down_ref[...] = dot(grad, emb_ref[...])


def last(back, ranks, proj, wdt, emb, grad_new):
    return pl.pallas_call(
        functools.partial(last_kernel, ranks.shape[0]),
        out_shape=(
            jax.ShapeDtypeStruct(grad_new.shape, F32),
            jax.ShapeDtypeStruct(wdt.shape, F32),
        ),
        in_specs=[VMEM] * 6,
        out_specs=(VMEM,) * 2,
        compiler_params=params(),
        name="last",
    )(back, ranks, proj, wdt, emb, grad_new)


def body(
    groups,
    members,
    edge_emb,
    atom_emb,
    edge_target,
    trip_in,
    trip_out,
    trip_count,
    trip_basis,
    grad_edge,
    grad_atom,
    w_down,
    w_bil,
    w_up,
    w_atom,
):
    emb = edge_emb[0]
    edges = emb.shape[0]
    atom_dev, wide = atom_emb.shape[1:]
    atoms = atom_dev * members
    far = members // NEAR
    wdt = w_down.T
    wbt = w_bil.T
    width = wdt.shape[0]
    basis = trip_basis[0]

    ranks, slots, proj, feat = names(trip_in, emb, wdt, members)
    wanted = exchange(ranks, ranks.shape, lead_block, lead_block, members, 1)
    chosen = select(wanted, feat)
    table = exchange(chosen, (far * width, NEAR * CAP), lead_block, tile_block, members, 2)
    total = forward(table, slots, trip_in, trip_out, trip_count, basis, edges)
    gathered, edge_new, slope, parts = edges_forward(total, wbt, w_up, emb, edge_target, atoms)
    parts = exchange(
        parts, (members, atom_dev, wide), functools.partial(row_block, atom_dev), lead_block, members, 3
    )
    atom_new, watom_term, grad_sum = atoms_step(parts, w_atom, atom_emb[0], grad_atom[0])
    grad_all = exchange(
        grad_sum, (atoms, wide), whole_block, functools.partial(row_block, atom_dev), members, 4
    )
    grad_new, wup_term, wbil_term, gg = turn(
        grad_all, edge_target, grad_edge[0], slope, w_up, gathered, total
    )
    sent = backward(gg, slots, trip_in, trip_out, trip_count, basis, w_bil, far)
    back = exchange(sent, (width, members * CAP), tile_block, lane_block, members, 5)
    grad_in, wdown_term = last(back, wanted, proj, wdt, emb, grad_new)
    down, bil, up, atom = lax.psum((wdown_term, wbil_term, wup_term, watom_term), ("dp", "graph"))
    factor = 1.0 / math.sqrt(groups * members * edges)
    return (
        edge_new[None],
        atom_new[None],
        grad_in[None],
        (down * factor).T,
        (bil * factor).T,
        up * factor,
        atom * factor,
    )


def solution(mesh):
    graph = P("dp", "graph")
    rows = P("dp", "graph", None)
    return jax.shard_map(
        functools.partial(body, mesh.shape["dp"], mesh.shape["graph"]),
        mesh=mesh,
        in_specs=(rows, rows, graph, graph, graph, graph, P("dp", None, "graph"), rows, rows)
        + (P(),) * 4,
        out_specs=(rows, rows, rows) + (P(),) * 4,
        check_vma=False,
    )
```

time: 571 us -> 347 us (0.61)
  other arithmetic: 185 us -> 4.72 us
  Pallas kernels: 0 us -> 176 us
  local copies, waits for them, and re-layouts: 124 us -> 0.86 us
  blocking collectives: 87 us -> 0 us
  waiting for transfers between devices: 72.3 us -> 150 us
  matrix products: 74.9 us -> 0 us
  starting transfers between devices: 21.1 us -> 0.04 us
  between operations: 1.67 us -> 14.7 us
    pallas_call x0 -> x13, Pallas kernels: none -> 176 us  [the longest x5 79 us: exchange(): pl.pallas_call(functools.partial(exchange_kernel, peers, source_at, targe...]
    psum x0 -> x1, waiting for transfers between devices: none -> 150 us  [body(): lax.psum((wdown_term, wbil_term, wup_term, watom_term), ('dp', 'graph'))]
    scatter-add x1 -> x0, other arithmetic: 91.3 us -> none  [body(): jax.ops.segment_sum(grad_feat_rows, incoming, num_segments=members * edge...]
    all_to_all x6 -> x0, blocking collectives: 87 us -> none  [the longest x3 49.8 us: sent_and_summed(): lax.all_to_all(in_blocks(value, dim, peers), axis, 0, 0, tiled=True)]
    dot_general x50 -> x0, matrix products: 74.9 us -> none  [the longest x8 28.9 us: backward_step(): lax.dot_general(spread, grad_part, contract_last, preferred_element_type=...]
    all_to_all x4 -> x0, waiting for transfers between devices: 72.3 us -> none  [the longest x3 44.6 us: from_everyone(): return lax.all_to_all(copies, axis, split_axis=0, concat_axis=0, tiled=True)]
    gather x2 -> x0, local copies, waits for them, and re-layouts: 60.1 us -> none  [the longest x1 58.1 us: body(): feat_in = jnp.take(edge_table_all, incoming, axis=0).T]
    convert_element_type x42 -> x0, other arithmetic: 39.2 us -> none  [the longest x16 15.9 us: spread_cols(): feat_part.astype(jnp.float32)[None, :, :]]
  transfers between devices with their start and end apart: 4 -> 1, of which waited for: 4 -> 1; matrix products, arithmetic and copies ran while one was open for 1% -> 0% of each run, Pallas kernels for 0% -> 0%
where the time goes in v1:
time: 347 us; the launch traced here: 346 us
  Pallas kernels  176 us (51%)
  waiting for transfers between devices  150 us (43%)
  between operations  14.7 us (4%)
  other arithmetic  4.72 us (1%)
    psum x1, waiting for transfers between devices, body(): lax.psum((wdown_term, wbil_term, wup_term, watom_term), ('dp', 'graph'))  150 us
    pallas_call x5, Pallas kernels, exchange(): pl.pallas_call(functools.partial(exchange_kernel, peers, source_at, targe...  79 us
    pallas_call x1, Pallas kernels, forward(): pl.pallas_call(functools.partial(forward_kernel, blocks, edges, far), gri...  32.4 us
    pallas_call x1, Pallas kernels, backward(): pl.pallas_call(functools.partial(backward_kernel, blocks, edges, far), gr...  25.7 us
    pallas_call x1, Pallas kernels, names(): pl.pallas_call(functools.partial(names_kernel, blocks, members), grid=(2...  10.6 us
    pallas_call x1, Pallas kernels, last(): pl.pallas_call(functools.partial(last_kernel, ranks.shape[0]), out_shape=...  8.26 us
    pallas_call x1, Pallas kernels, select(): pl.pallas_call(functools.partial(select_kernel, members), out_shape=jax.S...  7.41 us
  transfers between devices with their start and end apart: 1, of which 1 were waited for; matrix products, arithmetic and copies ran while one was open for 0% of the time, Pallas kernels for 0%

profile of v1, /device:TPU:1, one launch (start us, length us, event | category | flops | bytes accessed | tf_op | source)
XLA Modules:
  0.0 346.1 jit_solution(1355152442707262241)
XLA Ops:
  7.2 0.0 copy-start
  7.2 0.0 all-reduce.3.cloned.1.call-start
  7.2 10.6 %names.1 = (f32[32,4,128]{2,1,0:T(4,128)}, s32[1,16384]{1,0:T(1,128)}, f32[64,512]{1,0:T(8,128)}, bf16[64,512]{1,0:T(8,128)(2,1)}) custom-call(s32[1,16384]{1,0:T(1,128)} %in_ref.5, bf16[512,512]{1,0:T(8,128)(2,1)} %bitcast.14, bf16[64,512]{1,0:T(8,128)(2,1)} %bitcast.21), custom_call_target="tpu_custom_call" | custom-call | tf_op jit(solution)/shard_map/names/pallas_call | solution.py:191
  17.8 12.9 %exchange_1.1.rank_ref = f32[32,4,128]{2,1,0:T(4,128)} custom-call(f32[32,4,128]{2,1,0:T(4,128)} %get-tuple-element.24.x_ref), custom_call_target="tpu_custom_call" | custom-call | tf_op jit(solution)/shard_map/exchange_1/pallas_call | solution.py:97
  30.7 7.4 %select.1.x_ref = bf16[32,64,128]{2,1,0:T(8,128)(2,1)} custom-call(f32[32,4,128]{2,1,0:T(4,128)} %exchange_1.1.rank_ref, bf16[64,512]{1,0:T(8,128)(2,1)} %get-tuple-element.25.feat_ref), custom_call_target="tpu_custom_call" | custom-call | tf_op jit(solution)/shard_map/select/pallas_call | solution.py:236
  38.1 12.6 %exchange_2.1.table_ref = bf16[512,512]{1,0:T(8,128)(2,1)} custom-call(bf16[32,64,128]{2,1,0:T(8,128)(2,1)} %select.1.x_ref), custom_call_target="tpu_custom_call" | custom-call | tf_op jit(solution)/shard_map/exchange_2/pallas_call | solution.py:97
  51.4 0.0 copy-done
  51.4 0.8 copy.20.wbil_ref
  52.3 32.4 %forward.1.total_ref = f32[1024,512]{1,0:T(8,128)} custom-call(bf16[512,512]{1,0:T(8,128)(2,1)} %exchange_2.1.table_ref, s32[1,16384]{1,0:T(1,128)} %get-tuple-element.26.slot_ref, s32[1,16384]{1,0:T(1,128)} %in_ref.5, s32[1,16384]{1,0:T(1,128)} %out_ref.3, s32[1,1]{1,0:T(1,128)S(6)} %copy.25.count_ref, bf16[16,16384]{1,0:T(8,128)(2,1)} %bitcast.17), custom_call_target="tpu_custom_call" | custom-call | tf_op jit(solution)/shard_map/forward/pallas_call | solution.py:278
  84.6 4.5 %edges.1 = (bf16[64,512]{1,0:T(8,128)(2,1)}, bf16[512,512]{1,0:T(8,128)(2,1)}, f32[512,512]{1,0:T(8,128)}, bf16[1024,512]{1,0:T(8,128)(2,1)}) custom-call(f32[1024,512]{1,0:T(8,128)} %forward.1.total_ref, bf16[64,1024]{1,0:T(8,128)(2,1)} %bitcast.20, bf16[64,512]{1,0:T(8,128)(2,1)} %wup_ref.3, bf16[512,512]{1,0:T(8,128)(2,1)} %bitcast.15, s32[1,512]{1,0:T(1,128)} %target_ref.3), custom_call_target="tpu_custom_call" | custom-call | tf_op jit(solution)/shard_map/edges/pallas_call | solution.py:312
  89.1 19.1 %exchange_3.1.part_ref = bf16[32,32,512]{2,1,0:T(8,128)(2,1)} custom-call(bf16[1024,512]{1,0:T(8,128)(2,1)} %get-tuple-element.28.x_ref), custom_call_target="tpu_custom_call" | custom-call | tf_op jit(solution)/shard_map/exchange_3/pallas_call | solution.py:97
  108.2 3.0 atoms.1
  111.2 20.0 %exchange_4.1.all_ref = bf16[1024,512]{1,0:T(8,128)(2,1)} custom-call(bf16[32,512]{1,0:T(8,128)(2,1)} %get-tuple-element.30.x_ref), custom_call_target="tpu_custom_call" | custom-call | tf_op jit(solution)/shard_map/exchange_4/pallas_call | solution.py:97
  131.3 4.9 %turn.1 = (f32[512,512]{1,0:T(8,128)}, f32[64,512]{1,0:T(8,128)}, f32[64,1024]{1,0:T(8,128)}, bf16[64,512]{1,0:T(8,128)(2,1)}) custom-call(bf16[1024,512]{1,0:T(8,128)(2,1)} %exchange_4.1.all_ref, s32[1,512]{1,0:T(1,128)} %target_ref.3, bf16[512,512]{1,0:T(8,128)(2,1)} %bitcast.19, f32[512,512]{1,0:T(8,128)} %get-tuple-element.31.slope_ref, ...), custom_call_target="tpu_custom_call" | custom-call | tf_op jit(solution)/shard_map/turn/pallas_call | solution.py:366
  136.1 25.7 %backward.1.x_ref = bf16[512,512]{1,0:T(8,128)(2,1)} custom-call(bf16[64,512]{1,0:T(8,128)(2,1)} %get-tuple-element.33.gg_ref, s32[1,16384]{1,0:T(1,128)} %get-tuple-element.26.slot_ref, s32[1,16384]{1,0:T(1,128)} %in_ref.5, s32[1,16384]{1,0:T(1,128)} %out_ref.3, s32[1,1]{1,0:T(1,128)S(6)} %copy.25.count_ref, bf16[16,16384]{1,0:T(8,128)(2,1)} %bitcast.18, ...), custom_call_target="tpu_custom_call" | custom-call | tf_op jit(solution)/shard_map/backward/pallas_call | solution.py:418
  161.8 14.3 %exchange_5.1.back_ref = bf16[64,4096]{1,0:T(8,128)(2,1)} custom-call(bf16[512,512]{1,0:T(8,128)(2,1)} %backward.1.x_ref), custom_call_target="tpu_custom_call" | custom-call | tf_op jit(solution)/shard_map/exchange_5/pallas_call | solution.py:97
  176.1 8.3 %last.1 = (f32[512,512]{1,0:T(8,128)}, f32[64,512]{1,0:T(8,128)}) custom-call(bf16[64,4096]{1,0:T(8,128)(2,1)} %exchange_5.1.back_ref, f32[32,4,128]{2,1,0:T(4,128)} %exchange_1.1.rank_ref, f32[64,512]{1,0:T(8,128)} %get-tuple-element.34.proj_ref, bf16[64,512]{1,0:T(8,128)(2,1)} %bitcast.22, bf16[512,512]{1,0:T(8,128)(2,1)} %bitcast.16, ...), custom_call_target="tpu_custom_call" | custom-call | tf_op jit(solution)/shard_map/last/pallas_call | solution.py:450
  184.4 0.0 all-reduce.3.cloned.1.call-update
  184.4 150.1 %all-reduce.3.cloned.1.call-done = (f32[64,512]{1,0:T(8,128)}, f32[64,1024]{1,0:T(8,128)}, f32[64,512]{1,0:T(8,128)}, f32[512,512]{1,0:T(8,128)}) async-done(((f32[64,512]{1,0:T(8,128)}, f32[64,1024]{1,0:T(8,128)}, f32[64,512]{1,0:T(8,128)}, f32[512,512]{1,0:T(8,128)}), (f32[64,512]{1,0:T(8,128)}, f32[64,1024]{1,0:T(8,128)}, f32[64,512]{1,0:T(8,128)}, f32[512,512]{1,0:T(8,128)})) %all-reduce.3.cloned.1.call-update) | async-done | bytes 1572880 | tf_op jit(solution)/shard_map/psum | solution.py:509
  334.5 0.0 copy-start.1
  334.5 0.0 copy-start.2
  334.5 1.7 multiply_bitcast_fusion
  336.3 2.3 broadcast_multiply_fusion
  338.5 0.0 copy-done.1
  338.6 0.0 copy-done.2
  338.6 0.7 multiply_bitcast_fusion.1
Async XLA Ops:
  7.2 44.2 %copy-start = (bf16[1024,64]{0,1:T(8,128)(2,1)S(1)}, bf16[1024,64]{0,1:T(8,128)(2,1)}, u32[]{:S(2)}) copy-start(bf16[1024,64]{0,1:T(8,128)(2,1)} %param.23) | copy-start | bytes 393220
  7.2 327.4 %all-reduce.3.cloned.1.call-start = ((), (), s32[]{:S(2)}) async-start(), calls=%async_computation | async-start | bytes 3145728 | tf_op jit(solution)/shard_map/psum | solution.py:509
  334.5 4.0 %copy-start.1 = (f32[64,512]{1,0:T(8,128)S(1)}, f32[64,512]{1,0:T(8,128)}, u32[]{:S(2)}) copy-start(f32[64,512]{1,0:T(8,128)} %get-tuple-element.41) | copy-start | bytes 393220
  334.5 4.0 %copy-start.2 = (f32[64,512]{1,0:T(8,128)S(1)}, f32[64,512]{1,0:T(8,128)}, u32[]{:S(2)}) copy-start(f32[64,512]{1,0:T(8,128)} %get-tuple-element.43) | copy-start | bytes 393220
Sparse Core Ops, SparseCore 0:
  184.5 149.9 all-reduce.2

commit v2 on v1

v2 whole, which is shorter than its diff:
```python
import functools
import math

import jax
import jax.numpy as jnp
from jax import lax
from jax.experimental import pallas as pl
from jax.experimental.pallas import tpu as pltpu
from jax.sharding import PartitionSpec as P

MESH = pl.DeviceIdType.MESH
F32 = jnp.float32
BF16 = jnp.bfloat16
ATOM_SCALE = 0.25
CAP = 128
LANES = 128
NEAR = 4
BLOCK = 1024
ANY = pl.BlockSpec(memory_space=pl.ANY)
VMEM = pl.BlockSpec(memory_space=pltpu.VMEM)
NN = (((1,), (0,)), ((), ()))
NT = (((1,), (1,)), ((), ()))
TN = (((0,), (0,)), ((), ()))


def dot(a, b, dims=NN):
    return lax.dot_general(a, b, dims, preferred_element_type=F32)


def two_part_dot(a, b, dims=NN):
    high = a.astype(BF16)
    low = (a - high.astype(F32)).astype(BF16)
    return dot(high, b, dims) + dot(low, b, dims)


def rows_of(shape):
    return lax.broadcasted_iota(jnp.int32, shape, 0)


def hot(index, size):
    return (rows_of((size, index.shape[1])) == index).astype(F32).astype(BF16)


def silu_slope(value):
    logistic = jax.nn.sigmoid(value)
    return logistic * (1.0 + value * (1.0 - logistic))


def silu(value):
    return value * jax.nn.sigmoid(value)


def params(**kw):
    return pltpu.CompilerParams(vmem_limit_bytes=60 * 1024 * 1024, **kw)


def send_to(src, dst, send, recv, **where):
    return pltpu.make_async_remote_copy(
        src_ref=src,
        dst_ref=dst,
        send_sem=send,
        recv_sem=recv,
        device_id=where,
        device_id_type=MESH,
    )


def each(first, last, act):
    def one(k, c):
        act(k)
        return c

    lax.fori_loop(first, last, one, 0)


def some_rows(ref, index, rows):
    return ref.at[pl.ds(pl.multiple_of(index * rows, rows), rows), :]


def some_lanes(ref, index, lanes):
    return ref.at[:, pl.ds(pl.multiple_of(index * lanes, lanes), lanes)]


def tile_of(ref, row, rows, lane, lanes):
    return ref.at[
        pl.ds(pl.multiple_of(row * rows, rows), rows),
        pl.ds(pl.multiple_of(lane * lanes, lanes), lanes),
    ]


def greet(barrier, members, groups):
    me = lax.axis_index("graph")
    group = lax.axis_index("dp")
    each(
        1,
        members,
        lambda k: pl.semaphore_signal(
            barrier, inc=1, device_id={"graph": lax.rem(me + k, members)}, device_id_type=MESH
        ),
    )
    if groups > 1:
        each(
            1,
            groups,
            lambda k: pl.semaphore_signal(
                barrier, inc=1, device_id={"dp": lax.rem(group + k, groups)}, device_id_type=MESH
            ),
        )


def hot_of_ranks(rank_ref, hot_ref):
    members, per = rank_ref.shape[:2]
    place = lax.broadcasted_iota(jnp.int32, (CAP, LANES), 0).astype(F32)

    def one(d):
        ranks = rank_ref[d]
        at = pl.ds(pl.multiple_of(d * CAP, CAP), CAP)
        for q in range(per):
            hot_ref[at, q * LANES : (q + 1) * LANES] = (
                (place == ranks[q : q + 1, :]).astype(F32).astype(BF16)
            )

    each(0, members, one)


def early_kernel(
    members,
    far,
    in_ref,
    emb_ref,
    wdt_ref,
    wanted_ref,
    slot_ref,
    proj_ref,
    table_ref,
    table,
    found,
    rank_buf,
    hots,
    chosen,
    a_send,
    a_recv,
    b_send,
    b_recv,
):
    me = lax.axis_index("graph")
    barrier = pltpu.get_barrier_semaphore()
    greet(barrier, members, 1)
    highs = table.shape[0]
    per = highs // members
    width = wdt_ref.shape[0]
    block = math.gcd(in_ref.shape[1], 2 * BLOCK)
    blocks = in_ref.shape[1] // block

    def parts(i):
        index = in_ref[:, pl.ds(pl.multiple_of(i * block, block), block)]
        return lax.shift_right_logical(index, 7), lax.bitwise_and(index, LANES - 1)

    found[...] = jnp.zeros_like(found)

    def find(i):
        high, low = parts(i)
        found[...] += dot(hot(high, highs), hot(low, LANES), NT)

    each(0, blocks, find)
    there = jnp.where(found[...] > 0.0, 1.0, 0.0)
    there16 = there.astype(BF16)
    row = lax.broadcasted_iota(jnp.int32, (LANES, LANES), 0)
    col = lax.broadcasted_iota(jnp.int32, (LANES, LANES), 1)
    upper = (row <= col).astype(F32).astype(BF16)
    hrow = lax.broadcasted_iota(jnp.int32, (highs, highs), 0)
    hcol = lax.broadcasted_iota(jnp.int32, (highs, highs), 1)
    before = ((hcol < hrow) & (lax.div(hcol, per) == lax.div(hrow, per))).astype(F32).astype(BF16)
    ahead = dot(before, there16).astype(BF16)
    ones = jnp.ones((LANES, LANES), BF16)
    rank = dot(there16, upper) + dot(ahead, ones) - 1.0
    rank = jnp.where(there > 0.0, rank, -1.0)
    table[...] = rank.astype(BF16)
    for s in range(members):
        rank_buf[s] = rank[s * per : (s + 1) * per, :]
    proj = dot(wdt_ref[...], emb_ref[...], NT)
    proj_ref[...] = proj
    feat = silu(proj).astype(BF16)
    pl.semaphore_wait(barrier, members - 1)

    def rank_copy(k):
        peer = lax.rem(me + k, members)
        return send_to(rank_buf.at[peer], wanted_ref.at[me], a_send.at[k], a_recv.at[k], graph=peer)

    each(1, members, lambda k: rank_copy(k).start())
    wanted_ref[me] = rank_buf[me]

    def look(i):
        high, low = parts(i)
        ranks = dot(table[...], hot(high, highs), TN)
        picked = jnp.where(rows_of(ranks.shape) == low, ranks, 0.0)
        rank = jnp.sum(picked, axis=0, keepdims=True).astype(jnp.int32)
        near = lax.bitwise_and(lax.div(high, per), NEAR - 1)
        slot_ref[:, pl.ds(pl.multiple_of(i * block, block), block)] = near * CAP + rank

    each(0, blocks, look)
    each(1, members, lambda k: rank_copy(k).wait())
    hot_of_ranks(wanted_ref, hots)
    chosen[...] = dot(feat, hots[...], NT).astype(BF16)

    def place(ref, index):
        return tile_of(ref, lax.div(index, NEAR), width, lax.rem(index, NEAR), CAP)

    def feat_copy(k):
        peer = lax.rem(me + k, members)
        return send_to(
            some_lanes(chosen, peer, CAP), place(table_ref, me), b_send.at[k], b_recv.at[k], graph=peer
        )

    each(1, members, lambda k: feat_copy(k).start())
    place(table_ref, me)[...] = some_lanes(chosen, me, CAP)[...]
    each(1, members, lambda k: feat_copy(k).wait())


def early(incoming, emb, wdt, members):
    slots = incoming.shape[1]
    edges = emb.shape[0]
    width = wdt.shape[0]
    far = members // NEAR
    highs = members * edges // LANES
    per = highs // members
    return pl.pallas_call(
        functools.partial(early_kernel, members, far),
        out_shape=(
            jax.ShapeDtypeStruct((members, per, LANES), F32),
            jax.ShapeDtypeStruct((1, slots), jnp.int32),
            jax.ShapeDtypeStruct((width, edges), F32),
            jax.ShapeDtypeStruct((far * width, NEAR * CAP), BF16),
        ),
        in_specs=[VMEM] * 3,
        out_specs=(VMEM,) * 4,
        scratch_shapes=[
            pltpu.VMEM((highs, LANES), BF16),
            pltpu.VMEM((highs, LANES), F32),
            pltpu.VMEM((members, per, LANES), F32),
            pltpu.VMEM((members * CAP, edges), BF16),
            pltpu.VMEM((width, members * CAP), BF16),
        ]
        + [pltpu.SemaphoreType.DMA((members,))] * 4,
        compiler_params=params(collective_id=1, has_side_effects=True),
        name="early",
    )(incoming, emb, wdt)


def forward_kernel(
    blocks, edges, far, table_ref, slot_ref, in_ref, out_ref, count_ref, basis_ref, total_ref, spread
):
    step = pl.program_id(0)
    block = slot_ref.shape[1]
    width = table_ref.shape[0] // far
    shift = edges.bit_length() - 1 + NEAR.bit_length() - 1

    @pl.when(step == 0)
    def _():
        total_ref[...] = jnp.zeros_like(total_ref)

    group = lax.shift_right_logical(in_ref[...], shift)
    wide = dot(table_ref[...], hot(slot_ref[...], table_ref.shape[1]))
    feat = wide[0:width]
    for k in range(1, far):
        feat = jnp.where(group == k, wide[k * width : (k + 1) * width], feat)
    basis = basis_ref[...].astype(F32)
    for b in range(basis.shape[0]):
        spread[b * width : (b + 1) * width, :] = (basis[b : b + 1, :] * feat).astype(BF16)
    at = step * block + lax.broadcasted_iota(jnp.int32, (1, block), 1)
    place = jnp.where(at < count_ref[0, 0], out_ref[...], -1)
    total_ref[...] += dot(spread[...], hot(place, edges), NT)


def forward(table, slots, incoming, outgoing, count, basis, edges):
    total = slots.shape[1]
    block = math.gcd(total, BLOCK)
    blocks = total // block
    far = table.shape[0] // 64
    rows = basis.shape[0] * 64
    line = pl.BlockSpec((1, block), lambda i: (0, i))
    return pl.pallas_call(
        functools.partial(forward_kernel, blocks, edges, far),
        grid=(blocks,),
        out_shape=jax.ShapeDtypeStruct((rows, edges), F32),
        in_specs=[
            pl.BlockSpec(table.shape, lambda i: (0, 0)),
            line,
            line,
            line,
            pl.BlockSpec(memory_space=pltpu.SMEM),
            pl.BlockSpec((basis.shape[0], block), lambda i: (0, i)),
        ],
        out_specs=pl.BlockSpec((rows, edges), lambda i: (0, 0)),
        scratch_shapes=[pltpu.VMEM((rows, block), BF16)],
        compiler_params=params(),
        name="forward",
    )(table, slots, incoming, outgoing, count, basis)


def late_kernel(
    members,
    groups,
    far,
    scale,
    total_ref,
    wbt_ref,
    wup_ref,
    emb_ref,
    target_ref,
    watom_ref,
    atom_ref,
    gatom_ref,
    gedge_ref,
    slot_ref,
    in_ref,
    out_ref,
    count_ref,
    basis_ref,
    wbil_ref,
    wanted_ref,
    proj_ref,
    wdt_ref,
    new_ref,
    anew_ref,
    gin_ref,
    down_ref,
    bil_ref,
    up_ref,
    gat_ref,
    parts,
    half,
    pair,
    arrived,
    grads,
    slope,
    gnew,
    wa,
    wa_half,
    wa_pair,
    wa_in,
    wa_dp,
    wa_all,
    wb,
    wb_half,
    wb_pair,
    wb_in,
    wb_dp,
    wb_all,
    names,
    spread,
    sent,
    back,
    hots,
    wd,
    wd_in,
    wd_dp,
    wd_all,
    far_send,
    far_recv,
    duo_send,
    duo_recv,
    dp_send,
    dp_recv,
):
    me = lax.axis_index("graph")
    group = lax.axis_index("dp")
    chips = members // 2
    chip = lax.div(me, 2)
    core = lax.rem(me, 2)
    other = 1 - core
    partner = 2 * chip + other
    barrier = pltpu.get_barrier_semaphore()
    greet(barrier, members, groups)

    def chip_at(k):
        return lax.rem(chip + k, chips)

    def chip_from(k):
        return lax.rem(chip + chips - k, chips)

    def mine(c):
        return core * chips + c

    def theirs(c):
        return other * chips + c

    atom_dev, wide = atom_ref.shape
    edges = emb_ref.shape[0]
    width = wbt_ref.shape[0]
    total = total_ref[...]
    high = total.astype(BF16)
    low = (total - high.astype(F32)).astype(BF16)
    gathered = (dot(wbt_ref[...], high) + dot(wbt_ref[...], low)).astype(BF16)
    update = dot(gathered, wup_ref[...], TN)
    new = (emb_ref[...].astype(F32) + silu(update)).astype(BF16)
    new_ref[...] = new
    slope[...] = silu_slope(update)
    target = target_ref[...]
    shift = atom_dev.bit_length() - 1
    holder = lax.shift_right_logical(target, shift)
    line = lax.bitwise_and(holder, 1) * chips + lax.shift_right_logical(holder, 1)
    line = line * atom_dev + lax.bitwise_and(target, atom_dev - 1)
    parts[...] = dot(hot(line, parts.shape[0]), new).astype(BF16)
    pl.semaphore_wait(barrier, members - 1 + groups - 1)

    def pair_copy(k):
        c = chip_at(k)
        return send_to(
            some_rows(parts, theirs(c), atom_dev),
            some_rows(half, c, atom_dev),
            duo_send.at[0, k],
            duo_recv.at[0, k],
            graph=partner,
        )

    each(0, chips, lambda k: pair_copy(k).start())
    hot_of_ranks(wanted_ref, hots)

    def pair_sum(k):
        c = chip_at(k)
        pair_copy(k).wait_recv()
        return (
            some_rows(parts, mine(c), atom_dev)[...].astype(F32)
            + some_rows(half, c, atom_dev)[...].astype(F32)
        ).astype(BF16)

    def chip_copy(k):
        c = chip_at(k)
        return send_to(
            some_rows(pair, c, atom_dev), arrived.at[chip], far_send.at[0, k], far_recv.at[0, k], graph=2 * c + core
        )

    def pair_step(k):
        some_rows(pair, chip_at(k), atom_dev)[...] = pair_sum(k)
        chip_copy(k).start()

    each(1, chips, pair_step)
    arrived[chip] = pair_sum(0)
    each(1, chips, lambda k: chip_copy(k).wait_recv())

    asum = jnp.sum(arrived[...].astype(F32), axis=0).astype(BF16)
    pre = ATOM_SCALE * dot(asum, watom_ref[...])
    grad_pre = (gatom_ref[...].astype(F32) * silu_slope(pre)).astype(BF16)
    some_rows(grads, mine(chip), atom_dev)[...] = (
        ATOM_SCALE * dot(grad_pre, watom_ref[...], NT)
    ).astype(BF16)

    def grad_copy(k):
        rows = some_rows(grads, mine(chip), atom_dev)
        return send_to(rows, rows, far_send.at[1, k], far_recv.at[1, k], graph=2 * chip_at(k) + core)

    def grad_pass(k):
        rows = some_rows(grads, mine(chip_from(k)), atom_dev)
        return send_to(rows, rows, duo_send.at[1, k], duo_recv.at[1, k], graph=partner)

    def grad_forward(k):
        grad_copy(k).wait_recv()
        grad_pass(k).start()

    grad_pass(0).start()
    each(1, chips, lambda k: grad_copy(k).start())
    anew_ref[...] = (atom_ref[...].astype(F32) + silu(pre)).astype(BF16)
    wa[...] = (ATOM_SCALE * dot(asum, grad_pre, TN)).astype(BF16)
    each(1, chips, grad_forward)
    each(0, chips, lambda k: grad_pass(k).wait_recv())

    picked = dot(hot(line, grads.shape[0]), grads[...], TN)
    grad_new = gedge_ref[...].astype(F32) + picked
    gnew[...] = grad_new
    grad_update = (grad_new * slope[...]).astype(BF16)
    bil_wide = wbt_ref.shape[1]
    wb[:, bil_wide:] = dot(gathered, grad_update)
    gg = dot(wup_ref[...], grad_update, NT).astype(BF16)
    wb[:, :bil_wide] = dot(gg, high, NT) + dot(gg, low, NT)

    wa_rows = wa.shape[0] // members
    wb_rows = wb.shape[0] // 8
    wb_lanes = wb.shape[1] // NEAR
    wb_split = chips // NEAR

    def wb_tile(ref, c, base):
        return tile_of(ref, base * wb_split + lax.div(c, NEAR), wb_rows, lax.rem(c, NEAR), wb_lanes)

    def wa_duo():
        return send_to(
            some_rows(wa, other, wa.shape[0] // 2), wa_half, duo_send.at[2, 0], duo_recv.at[2, 0], graph=partner
        )

    def wb_duo():
        return send_to(
            some_rows(wb, other, wb.shape[0] // 2), wb_half, duo_send.at[2, 1], duo_recv.at[2, 1], graph=partner
        )

    def wa_far(k):
        c = chip_at(k)
        return send_to(
            some_rows(wa_pair, c, wa_rows), wa_in.at[chip], far_send.at[2, k], far_recv.at[2, k], graph=2 * c + core
        )

    def wb_far(k):
        c = chip_at(k)
        return send_to(
            wb_tile(wb_pair, c, 0), wb_in.at[chip], far_send.at[3, k], far_recv.at[3, k], graph=2 * c + core
        )

    def wa_group(k):
        peer = lax.rem(group + k, groups)
        return send_to(wa_dp.at[group], wa_dp.at[group], dp_send.at[0, k], dp_recv.at[0, k], dp=peer)

    def wb_group(k):
        peer = lax.rem(group + k, groups)
        return send_to(wb_dp.at[group], wb_dp.at[group], dp_send.at[1, k], dp_recv.at[1, k], dp=peer)

    def wa_back(k):
        rows = some_rows(wa_all, mine(chip), wa_rows)
        return send_to(rows, rows, far_send.at[4, k], far_recv.at[4, k], graph=2 * chip_at(k) + core)

    def wb_back(k):
        tile = wb_tile(wb_all, chip, core)
        return send_to(tile, tile, far_send.at[5, k], far_recv.at[5, k], graph=2 * chip_at(k) + core)

    def wa_pass(k):
        rows = some_rows(wa_all, mine(chip_from(k)), wa_rows)
        return send_to(rows, rows, duo_send.at[3, k], duo_recv.at[3, k], graph=partner)

    def wb_pass(k):
        tile = wb_tile(wb_all, chip_from(k), core)
        return send_to(tile, tile, duo_send.at[4, k], duo_recv.at[4, k], graph=partner)

    def sums_pair():
        wa_duo().wait_recv()
        wb_duo().wait_recv()
        wa_pair[...] = (
            some_rows(wa, core, wa.shape[0] // 2)[...].astype(F32) + wa_half[...].astype(F32)
        ).astype(BF16)
        wb_pair[...] = some_rows(wb, core, wb.shape[0] // 2)[...] + wb_half[...]

    def sums_far():
        def go(k):
            wa_far(k).start()
            wb_far(k).start()

        each(1, chips, go)
        wa_in[chip] = some_rows(wa_pair, chip, wa_rows)[...]
        wb_in[chip] = wb_tile(wb_pair, chip, 0)[...]

    def sums_group():
        def end(k):
            wa_far(k).wait_recv()
            wb_far(k).wait_recv()

        each(1, chips, end)
        wa_dp[group] = jnp.sum(wa_in[...].astype(F32), axis=0)
        wb_dp[group] = jnp.sum(wb_in[...], axis=0)

        def go(k):
            wa_group(k).start()
            wb_group(k).start()

        each(1, groups, go)

    def sums_back():
        def end(k):
            wa_group(k).wait_recv()
            wb_group(k).wait_recv()

        each(1, groups, end)
        some_rows(wa_all, mine(chip), wa_rows)[...] = (scale * jnp.sum(wa_dp[...], axis=0)).astype(BF16)
        wb_tile(wb_all, chip, core)[...] = scale * jnp.sum(wb_dp[...], axis=0)
        wa_pass(0).start()
        wb_pass(0).start()

        def go(k):
            wa_back(k).start()
            wb_back(k).start()

        each(1, chips, go)

    def sums_pass():
        def go(k):
            wa_back(k).wait_recv()
            wb_back(k).wait_recv()
            wa_pass(k).start()
            wb_pass(k).start()

        each(1, chips, go)

    wa_duo().start()
    wb_duo().start()

    block = math.gcd(slot_ref.shape[1], BLOCK)
    blocks = slot_ref.shape[1] // block
    far_shift = edges.bit_length() - 1 + NEAR.bit_length() - 1
    names[...] = jnp.zeros_like(names)
    acts = {1: sums_pair, 2: sums_far, 7: sums_group, 9: sums_back, 14: sums_pass}

    def triplets(i):
        for at, act in acts.items():
            pl.when(i == at * blocks // 16)(act)
        here = pl.ds(pl.multiple_of(i * block, block), block)
        at = i * block + lax.broadcasted_iota(jnp.int32, (1, block), 1)
        place = jnp.where(at < count_ref[0, 0], out_ref[:, here], -1)
        taken = dot(gg, hot(place, edges)).astype(BF16)
        backed = dot(wbil_ref[...], taken)
        basis = basis_ref[:, here].astype(F32)
        grad = basis[0:1, :] * backed[0:width]
        for b in range(1, basis.shape[0]):
            grad = grad + basis[b : b + 1, :] * backed[b * width : (b + 1) * width]
        source = lax.shift_right_logical(in_ref[:, here], far_shift)
        for k in range(far):
            spread[k * width : (k + 1) * width, :] = jnp.where(source == k, grad, 0.0).astype(BF16)
        names[...] += dot(spread[...], hot(slot_ref[:, here], names.shape[1]), NT)

    each(0, blocks, triplets)

    sent[...] = names[...].astype(BF16)

    def place(ref, index):
        return tile_of(ref, lax.div(index, NEAR), width, lax.rem(index, NEAR), CAP)

    def back_copy(k):
        peer = lax.rem(me + k, members)
        return send_to(
            place(sent, peer), some_lanes(back, me, CAP), far_send.at[6, k], far_recv.at[6, k], graph=peer
        )

    each(1, members, lambda k: back_copy(k).start())
    some_lanes(back, me, CAP)[...] = place(sent, me)[...]

    def sums_end(k):
        wa_pass(k).wait_recv()
        wb_pass(k).wait_recv()

    each(0, chips, sums_end)
    gat_ref[...] = wa_all[...].astype(F32)
    bil_ref[...] = wb_all[:, :bil_wide]
    up_ref[...] = wb_all[:, bil_wide:]
    each(1, members, lambda k: back_copy(k).wait_recv())
    grad = dot(back[...], hots[...])
    grad = (grad * silu_slope(proj_ref[...])).astype(BF16)

    wd[...] = dot(grad, emb_ref[...])

    def wd_tile(ref, index):
        return tile_of(ref, lax.div(index, NEAR), ref.shape[0] * NEAR // members, lax.rem(index, NEAR), LANES)

    def wd_far(k):
        peer = lax.rem(me + k, members)
        return send_to(wd_tile(wd, peer), wd_in.at[me], far_send.at[7, k], far_recv.at[7, k], graph=peer)

    def wd_group(k):
        peer = lax.rem(group + k, groups)
        return send_to(wd_dp.at[group], wd_dp.at[group], dp_send.at[2, k], dp_recv.at[2, k], dp=peer)

    def wd_back(k):
        tile = wd_tile(wd_all, me)
        return send_to(
            tile, tile, far_send.at[8, k], far_recv.at[8, k], graph=lax.rem(me + k, members)
        )

    each(1, members, lambda k: wd_far(k).start())
    wd_in[me] = wd_tile(wd, me)[...]
    gin_ref[...] = gnew[...] + dot(grad, wdt_ref[...], TN)
    each(1, members, lambda k: wd_far(k).wait_recv())
    wd_dp[group] = jnp.sum(wd_in[...], axis=0)
    each(1, groups, lambda k: wd_group(k).start())
    each(1, groups, lambda k: wd_group(k).wait_recv())
    wd_tile(wd_all, me)[...] = scale * jnp.sum(wd_dp[...], axis=0)
    each(1, members, lambda k: wd_back(k).start())

    def left(k):
        pair_copy(k).wait_send()
        grad_pass(k).wait_send()
        wa_pass(k).wait_send()
        wb_pass(k).wait_send()

    def left_far(k):
        chip_copy(k).wait_send()
        grad_copy(k).wait_send()
        wa_far(k).wait_send()
        wb_far(k).wait_send()
        wa_back(k).wait_send()
        wb_back(k).wait_send()

    def left_group(k):
        wa_group(k).wait_send()
        wb_group(k).wait_send()
        wd_group(k).wait_send()

    def left_all(k):
        back_copy(k).wait_send()
        wd_far(k).wait_send()

    each(0, chips, left)
    each(1, chips, left_far)
    each(1, groups, left_group)
    each(1, members, left_all)
    wa_duo().wait_send()
    wb_duo().wait_send()
    each(1, members, lambda k: wd_back(k).wait())
    down_ref[...] = wd_all[...]


def late(total, wbt, wup, emb, targets, watom, atom, gatom, gedge, slots, incoming, outgoing, count, basis, wbil, wanted, proj, wdt, members, groups, scale):
    edges, wide = emb.shape
    atom_dev = atom.shape[0]
    atoms = atom_dev * members
    width = wdt.shape[0]
    far = members // NEAR
    chips = members // 2
    block = math.gcd(slots.shape[1], BLOCK)
    all_wide = wbt.shape[1] + wide
    piece = (width // 8, all_wide // NEAR)
    wa_piece = (wide // members, wide)
    wd_piece = (width * NEAR // members, wide // NEAR)
    shape = jax.ShapeDtypeStruct
    return pl.pallas_call(
        functools.partial(late_kernel, members, groups, far, scale),
        out_shape=(
            shape((edges, wide), BF16),
            shape((atom_dev, wide), BF16),
            shape((edges, wide), F32),
            shape(wdt.shape, F32),
            shape(wbt.shape, F32),
            shape(wup.shape, F32),
            shape(watom.shape, F32),
        ),
        in_specs=[VMEM] * 12 + [pl.BlockSpec(memory_space=pltpu.SMEM)] + [VMEM] * 5,
        out_specs=(VMEM,) * 7,
        scratch_shapes=[
            pltpu.VMEM((atoms, wide), BF16),
            pltpu.VMEM((atoms // 2, wide), BF16),
            pltpu.VMEM((atoms // 2, wide), BF16),
            pltpu.VMEM((chips, atom_dev, wide), BF16),
            pltpu.VMEM((atoms, wide), BF16),
            pltpu.VMEM((edges, wide), F32),
            pltpu.VMEM((edges, wide), F32),
            pltpu.VMEM((wide, wide), BF16),
            pltpu.VMEM((wide // 2, wide), BF16),
            pltpu.VMEM((wide // 2, wide), BF16),
            pltpu.VMEM((chips, *wa_piece), BF16),
            pltpu.VMEM((groups, *wa_piece), F32),
            pltpu.VMEM((wide, wide), BF16),
            pltpu.VMEM((width, all_wide), F32),
            pltpu.VMEM((width // 2, all_wide), F32),
            pltpu.VMEM((width // 2, all_wide), F32),
            pltpu.VMEM((chips, *piece), F32),
            pltpu.VMEM((groups, *piece), F32),
            pltpu.VMEM((width, all_wide), F32),
            pltpu.VMEM((far * width, NEAR * CAP), F32),
            pltpu.VMEM((far * width, block), BF16),
            pltpu.VMEM((far * width, NEAR * CAP), BF16),
            pltpu.VMEM((width, members * CAP), BF16),
            pltpu.VMEM((members * CAP, edges), BF16),
            pltpu.VMEM((width, wide), F32),
            pltpu.VMEM((members, *wd_piece), F32),
            pltpu.VMEM((groups, *wd_piece), F32),
            pltpu.VMEM((width, wide), F32),
            pltpu.SemaphoreType.DMA((9, members)),
            pltpu.SemaphoreType.DMA((9, members)),
            pltpu.SemaphoreType.DMA((5, chips)),
            pltpu.SemaphoreType.DMA((5, chips)),
            pltpu.SemaphoreType.DMA((3, groups)),
            pltpu.SemaphoreType.DMA((3, groups)),
        ],
        compiler_params=params(collective_id=2, has_side_effects=True),
        name="late",
    )(total, wbt, wup, emb, targets, watom, atom, gatom, gedge, slots, incoming, outgoing, count, basis, wbil, wanted, proj, wdt)


def body(
    groups,
    members,
    edge_emb,
    atom_emb,
    edge_target,
    trip_in,
    trip_out,
    trip_count,
    trip_basis,
    grad_edge,
    grad_atom,
    w_down,
    w_bil,
    w_up,
    w_atom,
):
    emb = edge_emb[0]
    edges = emb.shape[0]
    wdt = w_down.T
    wbt = w_bil.T
    basis = trip_basis[0]
    wanted, slots, proj, table = early(trip_in, emb, wdt, members)
    total = forward(table, slots, trip_in, trip_out, trip_count, basis, edges)
    scale = 1.0 / math.sqrt(groups * members * edges)
    edge_new, atom_new, grad_in, down, bil, up, atom = late(
        total, wbt, w_up, emb, edge_target, w_atom, atom_emb[0], grad_atom[0], grad_edge[0],
        slots, trip_in, trip_out, trip_count, basis, w_bil, wanted, proj, wdt, members, groups, scale,
    )
    return (edge_new[None], atom_new[None], grad_in[None], down.T, bil.T, up, atom)


def solution(mesh):
    graph = P("dp", "graph")
    rows = P("dp", "graph", None)
    return jax.shard_map(
        functools.partial(body, mesh.shape["dp"], mesh.shape["graph"]),
        mesh=mesh,
        in_specs=(rows, rows, graph, graph, graph, graph, P("dp", None, "graph"), rows, rows)
        + (P(),) * 4,
        out_specs=(rows, rows, rows) + (P(),) * 4,
        check_vma=False,
    )
```

time: 347 us -> 158 us (0.46)
  waiting for transfers between devices: 150 us -> 0 us
  Pallas kernels: 176 us -> 146 us
  between operations: 14.7 us -> 1.33 us
  local copies, waits for them, and re-layouts: 0.86 us -> 10.4 us
  other arithmetic: 4.72 us -> 0 us
    psum x1 -> x0, waiting for transfers between devices: 150 us -> none  [body(): lax.psum((wdown_term, wbil_term, wup_term, watom_term), ('dp', 'graph'))]
    pallas_call x12 -> x2, Pallas kernels: 143 us -> 113 us  [the longest x1 87.3 us: late(): pl.pallas_call(functools.partial(late_kernel, members, groups, far, scale...]
    unnamed x7 -> x16, local copies, waits for them, and re-layouts: 0.86 us -> 10.4 us
  transfers between devices with their start and end apart: 1 -> 0, of which waited for: 1 -> 0; matrix products, arithmetic and copies ran while one was open for 0% -> 0% of each run, Pallas kernels for 0% -> 0%
where the time goes in v2:
time: 158 us
  Pallas kernels  146 us (92%)
  local copies, waits for them, and re-layouts  10.4 us (7%)
    pallas_call x1, Pallas kernels, late(): pl.pallas_call(functools.partial(late_kernel, members, groups, far, scale...  87.3 us
    pallas_call x1, Pallas kernels, forward(): pl.pallas_call(functools.partial(forward_kernel, blocks, edges, far), gri...  32.4 us
    pallas_call x1, Pallas kernels, early(): pl.pallas_call(functools.partial(early_kernel, members, far), out_shape=(...  26.2 us
    unnamed x16, local copies, waits for them, and re-layouts  10.4 us

profile of v2, /device:TPU:1, one launch (start us, length us, event | category | flops | bytes accessed | tf_op | source)
XLA Modules:
  0.0 157.6 jit_solution(15289771370452833956)
XLA Ops:
  1.3 1.7 %copy.20.wbil_ref = bf16[1024,64]{1,0:T(8,128)(2,1)} copy(bf16[1024,64]{0,1:T(8,128)(2,1)} %param.23) | data formatting | bytes 262144 | tf_op args[10]
  3.0 26.2 %early.1 = (f32[32,4,128]{2,1,0:T(4,128)}, s32[1,16384]{1,0:T(1,128)}, f32[64,512]{1,0:T(8,128)}, bf16[512,512]{1,0:T(8,128)(2,1)}) custom-call(s32[1,16384]{1,0:T(1,128)} %in_ref.5, bf16[512,512]{1,0:T(8,128)(2,1)} %bitcast.12, bf16[64,512]{1,0:T(8,128)(2,1)} %bitcast.20), custom_call_target="tpu_custom_call" | custom-call | tf_op jit(solution)/shard_map/early/pallas_call | solution.py:227
  29.3 32.4 %forward.1.total_ref = f32[1024,512]{1,0:T(8,128)} custom-call(bf16[512,512]{1,0:T(8,128)(2,1)} %get-tuple-element.18.table_ref, s32[1,16384]{1,0:T(1,128)} %get-tuple-element.19.slot_ref, s32[1,16384]{1,0:T(1,128)} %in_ref.5, s32[1,16384]{1,0:T(1,128)} %out_ref.3, s32[1,1]{1,0:T(1,128)S(6)} %copy.28.count_ref, bf16[16,16384]{1,0:T(8,128)(2,1)} %bitcast.14), custom_call_target="tpu_custom_call" | custom-call | tf_op jit(solution)/shard_map/forward/pallas_call | solution.py:282
  61.7 87.3 %late.1 = (bf16[512,512]{1,0:T(8,128)(2,1)}, bf16[32,512]{1,0:T(8,128)(2,1)}, f32[512,512]{1,0:T(8,128)}, f32[64,512]{1,0:T(8,128)}, f32[64,1024]{1,0:T(8,128)}, /*index=5*/f32[64,512]{1,0:T(8,128)}, f32[512,512]{1,0:T(8,128)}) custom-call(f32[1024,512]{1,0:T(8,128)} %forward.1.total_ref, bf16[64,1024]{1,0:T(8,128)(2,1)} %bitcast.18, ...), custom_call_target="tpu_custom_call" | custom-call | tf_op jit(solution)/shard_map/late/pallas_call | solution.py:718
  148.9 0.0 copy-start.3
  148.9 0.0 copy-start.1
  148.9 0.0 copy-start.2
  149.0 0.0 copy-start
  149.0 2.0 %copy.29 = bf16[1,512,512]{2,1,0:T(8,128)(2,1)} copy(bf16[1,512,512]{2,1,0:T(8,128)(2,1)} %bitcast.19) | data formatting | bytes 1048576
  151.0 1.4 copy.30
  152.3 2.3 %copy.31 = f32[1,512,512]{2,1,0:T(8,128)} copy(f32[1,512,512]{2,1,0:T(8,128)} %bitcast.16) | data formatting | bytes 2097152
  154.6 0.0 copy-done.3
  154.6 0.7 copy.32
  155.2 0.0 copy-done.1
  155.2 0.7 copy.33
  156.0 0.0 copy-done.2
  156.0 0.7 copy.34
  156.6 0.0 copy-done
  156.6 1.0 copy.35
Async XLA Ops:
  148.9 5.7 %copy-start.3 = (f32[64,512]{1,0:T(8,128)S(1)}, f32[64,512]{1,0:T(8,128)}, u32[]{:S(2)}) copy-start(f32[64,512]{1,0:T(8,128)} %get-tuple-element.25) | copy-start | bytes 393220
  148.9 6.3 %copy-start.1 = (f32[64,1024]{1,0:T(8,128)S(1)}, f32[64,1024]{1,0:T(8,128)}, u32[]{:S(2)}) copy-start(f32[64,1024]{1,0:T(8,128)} %get-tuple-element.26) | copy-start | bytes 786436
  148.9 7.0 %copy-start.2 = (f32[64,512]{1,0:T(8,128)S(1)}, f32[64,512]{1,0:T(8,128)}, u32[]{:S(2)}) copy-start(f32[64,512]{1,0:T(8,128)} %get-tuple-element.41) | copy-start | bytes 393220
  149.0 7.7 %copy-start = (f32[512,512]{1,0:T(8,128)S(1)}, f32[512,512]{1,0:T(8,128)}, u32[]{:S(2)}) copy-start(f32[512,512]{1,0:T(8,128)} %get-tuple-element.42) | copy-start | bytes 3145732

commit v3 on v0

v3 whole, which is shorter than its diff:
```python
import functools
import math

import jax
import jax.numpy as jnp
from jax import lax
from jax.experimental import pallas as pl
from jax.experimental.pallas import tpu as pltpu
from jax.sharding import PartitionSpec as P

MESH = pl.DeviceIdType.MESH
F32 = jnp.float32
BF16 = jnp.bfloat16
ATOM_SCALE = 0.25
CAP = 128
LANES = 128
NEAR_FORWARD = 2
NEAR_BACKWARD = 4
SPLIT = 4
BLOCK_NAMES = 2048
BLOCK_FORWARD = 2048
BLOCK_BACKWARD = 1024
ANY = pl.BlockSpec(memory_space=pl.ANY)
VMEM = pl.BlockSpec(memory_space=pltpu.VMEM)
NN = (((1,), (0,)), ((), ()))
NT = (((1,), (1,)), ((), ()))
TN = (((0,), (0,)), ((), ()))


def dot(a, b, dims=NN):
    return lax.dot_general(a, b, dims, preferred_element_type=F32)


def rows_of(shape):
    return lax.broadcasted_iota(jnp.int32, shape, 0)


def hot(index, size):
    return (rows_of((size, index.shape[1])) == index).astype(F32).astype(BF16)


def silu_slope(value):
    logistic = jax.nn.sigmoid(value)
    return logistic * (1.0 + value * (1.0 - logistic))


def silu(value):
    return value * jax.nn.sigmoid(value)


def params(**kw):
    return pltpu.CompilerParams(vmem_limit_bytes=60 * 1024 * 1024, **kw)


def send_to(src, dst, send, recv, **where):
    return pltpu.make_async_remote_copy(
        src_ref=src,
        dst_ref=dst,
        send_sem=send,
        recv_sem=recv,
        device_id=where,
        device_id_type=MESH,
    )


def drain(ref, sem):
    pltpu.make_async_copy(ref, ref, sem).wait()


def each(first, last, act, unroll=False):
    if unroll:
        for k in range(first, last):
            act(k)
        return

    def one(k, c):
        act(k)
        return c

    lax.fori_loop(first, last, one, 0)


def wrap(value, size):
    return jnp.where(value >= size, value - size, value)


def some_rows(ref, index, rows):
    return ref.at[pl.ds(pl.multiple_of(index * rows, rows), rows), :]


def some_lanes(ref, index, lanes):
    return ref.at[:, pl.ds(pl.multiple_of(index * lanes, lanes), lanes)]


def tile_of(ref, row, rows, lane, lanes):
    return ref.at[
        pl.ds(pl.multiple_of(row * rows, rows), rows),
        pl.ds(pl.multiple_of(lane * lanes, lanes), lanes),
    ]


def hot_of_ranks(rank_ref, hot_ref):
    members, per = rank_ref.shape[:2]
    place = lax.broadcasted_iota(jnp.int32, (CAP, LANES), 0).astype(F32)

    def one(d):
        ranks = rank_ref[d]
        at = pl.ds(pl.multiple_of(d * CAP, CAP), CAP)
        for q in range(per):
            hot_ref[at, q * LANES : (q + 1) * LANES] = (
                (place == ranks[q : q + 1, :]).astype(F32).astype(BF16)
            )

    each(0, members, one)


def block_kernel(members, groups, scale, names_of, *refs):
    r = dict(zip(names_of, refs))
    (in_ref, emb_ref, wdt_ref, wbt_ref, wup_ref, target_ref, atom_ref, gatom_ref, count_ref) = (
        r["incoming"], r["emb"], r["wdt"], r["wbt"], r["wup"], r["target"], r["atom"], r["gatom"], r["count"]
    )
    me = lax.axis_index("graph")
    group = lax.axis_index("dp")
    chips = members // 2
    chip = lax.div(me, 2)
    core = lax.rem(me, 2)
    other = 1 - core
    partner = 2 * chip + other
    all_send, all_recv, many_recv, dp_send, dp_recv, load = (
        r["all_send"], r["all_recv"], r["many_recv"], r["dp_send"], r["dp_recv"], r["load"]
    )

    def peer_at(k):
        return wrap(me + k, members)

    def chip_at(k):
        return wrap(chip + k, chips)

    def chip_from(k):
        return wrap(chip + chips - k, chips)

    def group_at(k):
        return wrap(group + k, groups)

    def mine(c):
        return core * chips + c

    loads = [
        pltpu.make_async_copy(r[name + "_hbm"], r[name], load.at[i])
        for i, name in enumerate(("outgoing", "basis", "watom", "gedge"))
    ]
    for one in loads:
        one.start()
    barrier = pltpu.get_barrier_semaphore()
    each(
        1,
        members,
        lambda k: pl.semaphore_signal(
            barrier, inc=1, device_id={"graph": peer_at(k)}, device_id_type=MESH
        ),
        True,
    )
    each(
        1,
        groups,
        lambda k: pl.semaphore_signal(
            barrier, inc=1, device_id={"dp": group_at(k)}, device_id_type=MESH
        ),
        True,
    )

    table, found, rank_buf, wanted, hots, chosen, name, features = (
        r["table"], r["found"], r["rank_buf"], r["wanted"], r["hots"], r["chosen"], r["name"], r["features"]
    )
    highs = table.shape[0]
    per = highs // members
    width = wdt_ref.shape[0]
    edges, wide = emb_ref.shape
    slots = in_ref.shape[1]
    nblock = math.gcd(slots, BLOCK_NAMES)

    def window(i, block):
        return pl.ds(pl.multiple_of(i * block, block), block)

    def parts_of(i):
        index = in_ref[:, window(i, nblock)]
        return lax.shift_right_logical(index, 7), lax.bitwise_and(index, LANES - 1)

    found[...] = jnp.zeros_like(found)

    def find(i):
        high, low = parts_of(i)
        found[...] += dot(hot(high, highs), hot(low, LANES), NT)

    each(0, slots // nblock, find)
    there = jnp.where(found[...] > 0.0, 1.0, 0.0)
    there16 = there.astype(BF16)
    row = lax.broadcasted_iota(jnp.int32, (LANES, LANES), 0)
    col = lax.broadcasted_iota(jnp.int32, (LANES, LANES), 1)
    upper = (row <= col).astype(F32).astype(BF16)
    hrow = lax.broadcasted_iota(jnp.int32, (highs, highs), 0)
    hcol = lax.broadcasted_iota(jnp.int32, (highs, highs), 1)
    before = ((hcol < hrow) & (lax.div(hcol, per) == lax.div(hrow, per))).astype(F32).astype(BF16)
    ahead = dot(before, there16).astype(BF16)
    ones = jnp.ones((LANES, LANES), BF16)
    rank = dot(there16, upper) + dot(ahead, ones) - 1.0
    rank = jnp.where(there > 0.0, rank, -1.0)
    table[...] = rank.astype(BF16)
    for s in range(members):
        rank_buf[s] = rank[s * per : (s + 1) * per, :]
    proj = dot(wdt_ref[...], emb_ref[...], NT)
    feat = silu(proj).astype(BF16)
    r["down_slope"][...] = silu_slope(proj)
    pl.semaphore_wait(barrier, members - 1 + groups - 1)

    def rank_copy(k):
        peer = peer_at(k)
        return send_to(rank_buf.at[peer], wanted.at[me], all_send.at[0], all_recv.at[0], graph=peer)

    each(1, members, lambda k: rank_copy(k).start(), True)
    wanted[me] = rank_buf[me]

    def look(i):
        high, low = parts_of(i)
        ranks = dot(table[...], hot(high, highs), TN)
        picked = jnp.where(rows_of(ranks.shape) == low, ranks, 0.0)
        rank = jnp.sum(picked, axis=0, keepdims=True).astype(jnp.int32)
        name[:, window(i, nblock)] = lax.div(high, per) * CAP + rank

    looks = slots // nblock
    each(0, looks // 2, look)
    drain(wanted.at[0 : members - 1], all_recv.at[0])
    hot_of_ranks(wanted, hots)
    chosen[...] = dot(feat, hots[...], NT).astype(BF16)

    def feature_tile(index):
        return tile_of(
            features, lax.div(index, NEAR_FORWARD), width, lax.rem(index, NEAR_FORWARD), CAP
        )

    def feature_copy(k):
        peer = peer_at(k)
        return send_to(
            some_lanes(chosen, peer, CAP), feature_tile(me), all_send.at[1], all_recv.at[1], graph=peer
        )

    each(1, members, lambda k: feature_copy(k).start(), True)
    feature_tile(me)[...] = some_lanes(chosen, me, CAP)[...]
    each(looks // 2, looks, look)
    r["wbil"][...] = wbt_ref[...].astype(F32).T.astype(BF16)
    drain(chosen.at[:, 0 : (members - 1) * CAP], all_recv.at[1])
    loads[0].wait()
    loads[1].wait()

    outgoing, basis_ref, spread, total_ref = r["outgoing"], r["basis"], r["spread"], r["total"]
    fblock = math.gcd(slots, BLOCK_FORWARD)
    far_shift = (NEAR_FORWARD * CAP).bit_length() - 1
    far = members // NEAR_FORWARD
    total_ref[...] = jnp.zeros_like(total_ref)

    def place_of(i, block):
        at = i * block + lax.broadcasted_iota(jnp.int32, (1, block), 1)
        return jnp.where(at < count_ref[0, 0], outgoing[:, window(i, block)], -1)

    def forward(i):
        here = window(i, fblock)
        index = name[:, here]
        group_of = lax.shift_right_logical(index, far_shift)
        all_wide = dot(features[...], hot(lax.bitwise_and(index, NEAR_FORWARD * CAP - 1), NEAR_FORWARD * CAP))
        feat = all_wide[0:width]
        for k in range(1, far):
            feat = jnp.where(group_of == k, all_wide[k * width : (k + 1) * width], feat)
        basis = basis_ref[:, here].astype(F32)
        for b in range(basis.shape[0]):
            spread[b * width : (b + 1) * width, :] = (basis[b : b + 1, :] * feat).astype(BF16)
        total_ref[...] += dot(spread[...], hot(place_of(i, fblock), edges), NT)

    each(0, slots // fblock, forward)

    parts, half, pair, arrived, grads, slope, gnew = (
        r["parts"], r["half"], r["pair"], r["arrived"], r["grads"], r["slope"], r["gnew"]
    )
    new_ref, anew_ref = r["new_out"], r["anew_out"]
    atom_dev = atom_ref.shape[0]
    total = total_ref[...]
    high = total.astype(BF16)
    low = (total - high.astype(F32)).astype(BF16)
    gathered = (dot(wbt_ref[...], high) + dot(wbt_ref[...], low)).astype(BF16)
    target = target_ref[...]
    holder = lax.shift_right_logical(target, atom_dev.bit_length() - 1)
    line = lax.bitwise_and(holder, 1) * chips + lax.shift_right_logical(holder, 1)
    line = line * atom_dev + lax.bitwise_and(target, atom_dev - 1)
    line_hot = hot(line, parts.shape[0])
    part = wide // SPLIT

    def pair_copy(q):
        rows = parts.shape[0] // 2
        lanes = slice(q * part, (q + 1) * part)
        return send_to(
            parts.at[pl.ds(pl.multiple_of(other * rows, rows), rows), lanes],
            half.at[:, lanes],
            all_send.at[2],
            many_recv.at[0, q],
            graph=partner,
        )

    for q in range(SPLIT):
        lanes = slice(q * part, (q + 1) * part)
        update = dot(gathered, wup_ref[:, lanes], TN)
        new = (emb_ref[:, lanes].astype(F32) + silu(update)).astype(BF16)
        new_ref[:, lanes] = new
        slope[:, lanes] = silu_slope(update)
        parts[:, lanes] = dot(line_hot, new).astype(BF16)
        pair_copy(q).start()

    def chip_copy(k):
        c = chip_at(k)
        return send_to(
            some_rows(pair, c, atom_dev), arrived.at[chip], all_send.at[3], all_recv.at[3], graph=2 * c + core
        )

    for q in range(SPLIT):
        lanes = slice(q * part, (q + 1) * part)
        rows = parts.shape[0] // 2
        own = parts[pl.ds(pl.multiple_of(core * rows, rows), rows), lanes].astype(F32)
        pair_copy(q).wait_recv()
        pair[:, lanes] = (own + half[:, lanes].astype(F32)).astype(BF16)
    each(1, chips, lambda k: chip_copy(k).start(), True)
    arrived[chip] = some_rows(pair, chip, atom_dev)[...]
    loads[2].wait()
    loads[3].wait()
    watom_ref, gedge_ref = r["watom"], r["gedge"]
    drain(arrived.at[0 : chips - 1], all_recv.at[3])

    asum = jnp.sum(arrived[...].astype(F32), axis=0).astype(BF16)
    pre = ATOM_SCALE * dot(asum, watom_ref[...])
    grad_pre = (gatom_ref[...].astype(F32) * silu_slope(pre)).astype(BF16)
    some_rows(grads, mine(chip), atom_dev)[...] = (
        ATOM_SCALE * dot(grad_pre, watom_ref[...], NT)
    ).astype(BF16)

    def grad_copy(k):
        rows = some_rows(grads, mine(chip), atom_dev)
        return send_to(rows, rows, all_send.at[4], many_recv.at[1, k], graph=2 * chip_at(k) + core)

    def grad_pass(k):
        rows = some_rows(grads, mine(chip_from(k)), atom_dev)
        return send_to(rows, rows, all_send.at[5], all_recv.at[5], graph=partner)

    def grad_forward(k):
        grad_copy(k).wait_recv()
        grad_pass(k).start()

    each(1, chips, lambda k: grad_copy(k).start(), True)
    grad_pass(0).start()
    wa, wb = r["wa"], r["wb"]
    anew_ref[...] = (atom_ref[...].astype(F32) + silu(pre)).astype(BF16)
    wa[...] = (ATOM_SCALE * dot(asum, grad_pre, TN)).astype(BF16)
    each(1, chips, grad_forward, True)
    drain(half, all_recv.at[5])

    picked = dot(hot(line, grads.shape[0]), grads[...], TN)
    grad_new = gedge_ref[...].astype(F32) + picked
    gnew[...] = grad_new
    grad_update = (grad_new * slope[...]).astype(BF16)
    bil_wide = wbt_ref.shape[1]
    wb[:, bil_wide:] = dot(gathered, grad_update)
    gg = dot(wup_ref[...], grad_update, NT).astype(BF16)
    wb[:, :bil_wide] = dot(gg, high, NT) + dot(gg, low, NT)

    wa_half, wa_pair, wa_in, wa_dp, wa_all = r["wa_half"], r["wa_pair"], r["wa_in"], r["wa_dp"], r["wa_out"]
    wb_half, wb_pair, wb_in, wb_dp, wb_all = r["wb_half"], r["wb_pair"], r["wb_in"], r["wb_dp"], r["wb_out"]
    wa_rows = wa.shape[0] // members
    wb_rows = wb.shape[0] // 8
    wb_lanes = wb.shape[1] // SPLIT
    wb_split = chips // SPLIT

    def wb_tile(ref, c, base):
        return tile_of(ref, base * wb_split + lax.div(c, SPLIT), wb_rows, lax.rem(c, SPLIT), wb_lanes)

    def wa_duo():
        return send_to(
            some_rows(wa, other, wa.shape[0] // 2), wa_half, all_send.at[6], all_recv.at[6], graph=partner
        )

    def wb_duo():
        return send_to(
            some_rows(wb, other, wb.shape[0] // 2), wb_half, all_send.at[7], all_recv.at[7], graph=partner
        )

    def wa_far(k):
        c = chip_at(k)
        return send_to(
            some_rows(wa_pair, c, wa_rows), wa_in.at[chip], all_send.at[8], all_recv.at[8], graph=2 * c + core
        )

    def wb_far(k):
        c = chip_at(k)
        return send_to(
            wb_tile(wb_pair, c, 0), wb_in.at[chip], all_send.at[9], all_recv.at[9], graph=2 * c + core
        )

    def wa_group(k):
        return send_to(wa_dp.at[group], wa_dp.at[group], dp_send.at[0], dp_recv.at[0], dp=group_at(k))

    def wb_group(k):
        return send_to(wb_dp.at[group], wb_dp.at[group], dp_send.at[1], dp_recv.at[1], dp=group_at(k))

    def wa_back(k):
        rows = some_rows(wa_all, mine(chip), wa_rows)
        return send_to(rows, rows, all_send.at[10], all_recv.at[10], graph=2 * chip_at(k) + core)

    def wb_back(k):
        tile = wb_tile(wb_all, chip, core)
        return send_to(tile, tile, all_send.at[11], all_recv.at[11], graph=2 * chip_at(k) + core)

    def wa_pass():
        rows = some_rows(wa_all, core, wa.shape[0] // 2)
        return send_to(rows, rows, all_send.at[12], all_recv.at[12], graph=partner)

    def wb_pass():
        rows = some_rows(wb_all, core, wb.shape[0] // 2)
        return send_to(rows, rows, all_send.at[13], all_recv.at[13], graph=partner)

    def sums_pair():
        wa_duo().wait_recv()
        wb_duo().wait_recv()
        wa_pair[...] = (
            some_rows(wa, core, wa.shape[0] // 2)[...].astype(F32) + wa_half[...].astype(F32)
        ).astype(BF16)
        wb_pair[...] = some_rows(wb, core, wb.shape[0] // 2)[...] + wb_half[...]

    def sums_far():
        def go(k):
            wa_far(k).start()
            wb_far(k).start()

        each(1, chips, go, True)
        wa_in[chip] = some_rows(wa_pair, chip, wa_rows)[...]
        wb_in[chip] = wb_tile(wb_pair, chip, 0)[...]

    def sums_group():
        drain(wa_in.at[0 : chips - 1], all_recv.at[8])
        drain(wb_in.at[0 : chips - 1], all_recv.at[9])
        wa_dp[group] = jnp.sum(wa_in[...].astype(F32), axis=0)
        wb_dp[group] = jnp.sum(wb_in[...], axis=0)

        def go(k):
            wa_group(k).start()
            wb_group(k).start()

        each(1, groups, go, True)

    def sums_back():
        drain(wa_dp.at[0 : groups - 1], dp_recv.at[0])
        drain(wb_dp.at[0 : groups - 1], dp_recv.at[1])
        some_rows(wa_all, mine(chip), wa_rows)[...] = (scale * jnp.sum(wa_dp[...], axis=0)).astype(BF16)
        wb_tile(wb_all, chip, core)[...] = scale * jnp.sum(wb_dp[...], axis=0)

        def go(k):
            wa_back(k).start()
            wb_back(k).start()

        each(1, chips, go, True)

    def sums_pass():
        drain(wa_in.at[0 : chips - 1], all_recv.at[10])
        drain(wb_in.at[0 : chips - 1], all_recv.at[11])
        wa_pass().start()
        wb_pass().start()

    wa_duo().start()
    wb_duo().start()

    sent, back = r["sent"], r["back"]
    named, masked, wbil = r["named"], r["masked"], r["wbil"]
    block = math.gcd(slots, BLOCK_BACKWARD)
    blocks = slots // block
    back_far = members // NEAR_BACKWARD
    back_shift = (NEAR_BACKWARD * CAP).bit_length() - 1
    named[...] = jnp.zeros_like(named)
    acts = {1: sums_pair, 2: sums_far, 7: sums_group, 9: sums_back, 14: sums_pass}

    def backward(i):
        for at, act in acts.items():
            pl.when(i == at * blocks // 16)(act)
        here = window(i, block)
        taken = dot(gg, hot(place_of(i, block), edges)).astype(BF16)
        backed = dot(wbil[...], taken)
        basis = basis_ref[:, here].astype(F32)
        grad = basis[0:1, :] * backed[0:width]
        for b in range(1, basis.shape[0]):
            grad = grad + basis[b : b + 1, :] * backed[b * width : (b + 1) * width]
        index = name[:, here]
        source = lax.shift_right_logical(index, back_shift)
        for k in range(back_far):
            masked[k * width : (k + 1) * width, :] = jnp.where(source == k, grad, 0.0).astype(BF16)
        near = lax.bitwise_and(index, NEAR_BACKWARD * CAP - 1)
        named[...] += dot(masked[...], hot(near, NEAR_BACKWARD * CAP), NT)

    each(0, blocks, backward)

    sent[...] = named[...].astype(BF16)

    def sent_tile(index):
        return tile_of(sent, lax.div(index, NEAR_BACKWARD), width, lax.rem(index, NEAR_BACKWARD), CAP)

    def back_copy(k):
        peer = peer_at(k)
        return send_to(
            sent_tile(peer), some_lanes(back, me, CAP), all_send.at[14], all_recv.at[14], graph=peer
        )

    each(1, members, lambda k: back_copy(k).start(), True)
    some_lanes(back, me, CAP)[...] = sent_tile(me)[...]
    wa_pass().wait_recv()
    wb_pass().wait_recv()
    drain(back.at[:, 0 : (members - 1) * CAP], all_recv.at[14])
    grad = dot(back[...], hots[...])
    grad = (grad * r["down_slope"][...]).astype(BF16)

    wd, wd_in, wd_dp, wd_all = r["wd"], r["wd_in"], r["wd_dp"], r["wd_out"]
    wd[...] = dot(grad, emb_ref[...])

    def wd_tile(ref, index):
        return tile_of(ref, lax.div(index, SPLIT), ref.shape[0] * SPLIT // members, lax.rem(index, SPLIT), LANES)

    def wd_far(k):
        peer = peer_at(k)
        return send_to(wd_tile(wd, peer), wd_in.at[me], all_send.at[15], all_recv.at[15], graph=peer)

    def wd_group(k):
        return send_to(wd_dp.at[group], wd_dp.at[group], dp_send.at[2], dp_recv.at[2], dp=group_at(k))

    def wd_back(k):
        tile = wd_tile(wd_all, me)
        return send_to(tile, tile, all_send.at[16], all_recv.at[16], graph=peer_at(k))

    each(1, members, lambda k: wd_far(k).start(), True)
    wd_in[me] = wd_tile(wd, me)[...]
    r["gin_out"][...] = gnew[...] + dot(grad, wdt_ref[...], TN)
    drain(wd_in.at[0 : members - 1], all_recv.at[15])
    wd_dp[group] = jnp.sum(wd_in[...], axis=0)
    each(1, groups, lambda k: wd_group(k).start(), True)
    drain(wd_dp.at[0 : groups - 1], dp_recv.at[2])
    wd_tile(wd_all, me)[...] = scale * jnp.sum(wd_dp[...], axis=0)
    each(1, members, lambda k: wd_back(k).start(), True)

    drain(wanted.at[0 : members - 1], all_send.at[0])
    drain(chosen.at[:, 0 : (members - 1) * CAP], all_send.at[1])
    drain(half, all_send.at[2])
    drain(arrived.at[0 : chips - 1], all_send.at[3])
    drain(arrived.at[0 : chips - 1], all_send.at[4])
    drain(half, all_send.at[5])
    wa_duo().wait_send()
    wb_duo().wait_send()
    drain(wa_in.at[0 : chips - 1], all_send.at[8])
    drain(wb_in.at[0 : chips - 1], all_send.at[9])
    drain(wa_in.at[0 : chips - 1], all_send.at[10])
    drain(wb_in.at[0 : chips - 1], all_send.at[11])
    wa_pass().wait_send()
    wb_pass().wait_send()
    drain(wa_dp.at[0 : groups - 1], dp_send.at[0])
    drain(wb_dp.at[0 : groups - 1], dp_send.at[1])
    drain(wd_dp.at[0 : groups - 1], dp_send.at[2])
    drain(back.at[:, 0 : (members - 1) * CAP], all_send.at[14])
    drain(wd_in.at[0 : members - 1], all_send.at[15])
    drain(wd_in.at[0 : members - 1], all_send.at[16])
    drain(wd_in.at[0 : members - 1], all_recv.at[16])


def block_of(values, members, groups, scale):
    shape = jax.ShapeDtypeStruct
    edges, wide = values["emb"].shape
    atom_dev = values["atom"].shape[0]
    atoms = atom_dev * members
    width = values["wdt"].shape[0]
    slots = values["incoming"].shape[1]
    rows = values["wbt"].shape[1]
    chips = members // 2
    highs = members * edges // LANES
    per = highs // members
    all_wide = rows + wide
    piece = (width // 8, all_wide // SPLIT)
    wa_piece = (wide // members, wide)
    wd_piece = (width * SPLIT // members, wide // SPLIT)
    far = members // NEAR_FORWARD
    back_far = members // NEAR_BACKWARD
    late = ("outgoing", "basis", "watom", "gedge")
    ins, specs, args = [], [], []
    for key, value in values.items():
        if key in late:
            ins.append(key + "_hbm")
            specs.append(ANY)
        else:
            ins.append(key)
            specs.append(pl.BlockSpec(memory_space=pltpu.SMEM) if key == "count" else VMEM)
        args.append(value)
    outs = {
        "new_out": shape((edges, wide), BF16),
        "anew_out": shape((atom_dev, wide), BF16),
        "gin_out": shape((edges, wide), F32),
        "wa_out": shape((wide, wide), BF16),
        "wb_out": shape((width, all_wide), F32),
        "wd_out": shape((width, wide), F32),
    }
    scratch = {key: pltpu.VMEM(values[key].shape, values[key].dtype) for key in late}
    scratch |= {
        "table": pltpu.VMEM((highs, LANES), BF16),
        "found": pltpu.VMEM((highs, LANES), F32),
        "rank_buf": pltpu.VMEM((members, per, LANES), F32),
        "wanted": pltpu.VMEM((members, per, LANES), F32),
        "hots": pltpu.VMEM((members * CAP, edges), BF16),
        "chosen": pltpu.VMEM((width, members * CAP), BF16),
        "name": pltpu.VMEM((1, slots), jnp.int32),
        "features": pltpu.VMEM((far * width, NEAR_FORWARD * CAP), BF16),
        "down_slope": pltpu.VMEM((width, edges), F32),
        "wbil": pltpu.VMEM((rows, width), BF16),
        "spread": pltpu.VMEM((rows, math.gcd(slots, BLOCK_FORWARD)), BF16),
        "total": pltpu.VMEM((rows, edges), F32),
        "parts": pltpu.VMEM((atoms, wide), BF16),
        "half": pltpu.VMEM((atoms // 2, wide), BF16),
        "pair": pltpu.VMEM((atoms // 2, wide), BF16),
        "arrived": pltpu.VMEM((chips, atom_dev, wide), BF16),
        "grads": pltpu.VMEM((atoms, wide), BF16),
        "slope": pltpu.VMEM((edges, wide), F32),
        "gnew": pltpu.VMEM((edges, wide), F32),
        "wa": pltpu.VMEM((wide, wide), BF16),
        "wa_half": pltpu.VMEM((wide // 2, wide), BF16),
        "wa_pair": pltpu.VMEM((wide // 2, wide), BF16),
        "wa_in": pltpu.VMEM((chips, *wa_piece), BF16),
        "wa_dp": pltpu.VMEM((groups, *wa_piece), F32),
        "wb": pltpu.VMEM((width, all_wide), F32),
        "wb_half": pltpu.VMEM((width // 2, all_wide), F32),
        "wb_pair": pltpu.VMEM((width // 2, all_wide), F32),
        "wb_in": pltpu.VMEM((chips, *piece), F32),
        "wb_dp": pltpu.VMEM((groups, *piece), F32),
        "named": pltpu.VMEM((back_far * width, NEAR_BACKWARD * CAP), F32),
        "masked": pltpu.VMEM((back_far * width, math.gcd(slots, BLOCK_BACKWARD)), BF16),
        "sent": pltpu.VMEM((back_far * width, NEAR_BACKWARD * CAP), BF16),
        "back": pltpu.VMEM((width, members * CAP), BF16),
        "wd": pltpu.VMEM((width, wide), F32),
        "wd_in": pltpu.VMEM((members, *wd_piece), F32),
        "wd_dp": pltpu.VMEM((groups, *wd_piece), F32),
        "all_send": pltpu.SemaphoreType.DMA((17,)),
        "all_recv": pltpu.SemaphoreType.DMA((17,)),
        "many_recv": pltpu.SemaphoreType.DMA((2, chips)),
        "dp_send": pltpu.SemaphoreType.DMA((3,)),
        "dp_recv": pltpu.SemaphoreType.DMA((3,)),
        "load": pltpu.SemaphoreType.DMA((4,)),
    }
    return pl.pallas_call(
        functools.partial(block_kernel, members, groups, scale, (*ins, *outs, *scratch)),
        out_shape=tuple(outs.values()),
        in_specs=specs,
        out_specs=(VMEM,) * len(outs),
        scratch_shapes=list(scratch.values()),
        compiler_params=params(collective_id=1, has_side_effects=True),
        name="block",
    )(*args)


def finish_kernel(*refs):
    new, anew, gin, wa, wb, wd, new_o, anew_o, gin_o, down_o, bil_o, up_o, gat_o = refs
    new_o[...] = new[...]
    anew_o[...] = anew[...]
    gin_o[...] = gin[...]
    down_o[...] = wd[...]
    bil_o[...] = wb[:, : bil_o.shape[1]]
    up_o[...] = wb[:, bil_o.shape[1] :]
    gat_o[...] = wa[...].astype(F32)


def finish(new, anew, gin, wa, wb, wd):
    shape = jax.ShapeDtypeStruct
    wide = wa.shape[1]
    width = wb.shape[0]
    return pl.pallas_call(
        finish_kernel,
        out_shape=(
            shape(new.shape, BF16),
            shape(anew.shape, BF16),
            shape(gin.shape, F32),
            shape(wd.shape, F32),
            shape((width, wb.shape[1] - wide), F32),
            shape((width, wide), F32),
            shape(wa.shape, F32),
        ),
        in_specs=[VMEM] * 6,
        out_specs=(VMEM,) * 7,
        compiler_params=params(),
        name="finish",
    )(new, anew, gin, wa, wb, wd)


def body(
    groups,
    members,
    edge_emb,
    atom_emb,
    edge_target,
    trip_in,
    trip_out,
    trip_count,
    trip_basis,
    grad_edge,
    grad_atom,
    w_down,
    w_bil,
    w_up,
    w_atom,
):
    scale = 1.0 / math.sqrt(groups * members * edge_emb.shape[1])
    values = dict(
        incoming=trip_in,
        emb=edge_emb[0],
        wdt=w_down.T,
        wbt=w_bil.T,
        wup=w_up,
        target=edge_target,
        atom=atom_emb[0],
        gatom=grad_atom[0],
        count=trip_count,
        outgoing=trip_out,
        basis=trip_basis[0],
        watom=w_atom,
        gedge=grad_edge[0],
    )
    edge_new, atom_new, grad_in, down, bil, up, atom = finish(*block_of(values, members, groups, scale))
    return (edge_new[None], atom_new[None], grad_in[None], down.T, bil.T, up, atom)


def solution(mesh):
    graph = P("dp", "graph")
    rows = P("dp", "graph", None)
    return jax.shard_map(
        functools.partial(body, mesh.shape["dp"], mesh.shape["graph"]),
        mesh=mesh,
        in_specs=(rows, rows, graph, graph, graph, graph, P("dp", None, "graph"), rows, rows)
        + (P(),) * 4,
        out_specs=(rows, rows, rows) + (P(),) * 4,
        check_vma=False,
    )
```

time: 571 us -> 135 us (0.24)
  other arithmetic: 185 us -> 0 us
  Pallas kernels: 0 us -> 134 us
  local copies, waits for them, and re-layouts: 124 us -> 0 us
  blocking collectives: 87 us -> 0 us
  matrix products: 74.9 us -> 0 us
  waiting for transfers between devices: 72.3 us -> 0 us
  starting transfers between devices: 21.1 us -> 0 us
    pallas_call x0 -> x2, Pallas kernels: none -> 134 us  [the longest x1 131 us: block_of(): pl.pallas_call(functools.partial(block_kernel, members, groups, scale, (*...]
    scatter-add x1 -> x0, other arithmetic: 91.3 us -> none  [body(): jax.ops.segment_sum(grad_feat_rows, incoming, num_segments=members * edge...]
    all_to_all x6 -> x0, blocking collectives: 87 us -> none  [the longest x3 49.8 us: sent_and_summed(): lax.all_to_all(in_blocks(value, dim, peers), axis, 0, 0, tiled=True)]
    dot_general x50 -> x0, matrix products: 74.9 us -> none  [the longest x8 28.9 us: backward_step(): lax.dot_general(spread, grad_part, contract_last, preferred_element_type=...]
    all_to_all x4 -> x0, waiting for transfers between devices: 72.3 us -> none  [the longest x3 44.6 us: from_everyone(): return lax.all_to_all(copies, axis, split_axis=0, concat_axis=0, tiled=True)]
    gather x2 -> x0, local copies, waits for them, and re-layouts: 60.1 us -> none  [the longest x1 58.1 us: body(): feat_in = jnp.take(edge_table_all, incoming, axis=0).T]
    convert_element_type x42 -> x0, other arithmetic: 39.2 us -> none  [the longest x16 15.9 us: spread_cols(): feat_part.astype(jnp.float32)[None, :, :]]
    reduce_sum x13 -> x0, other arithmetic: 34.8 us -> none  [the longest x8 27.2 us: backward_step(): jnp.sum(basis_part.astype(jnp.float32)[:, None, :] * backed, axis=0)]
  transfers between devices with their start and end apart: 4 -> 0, of which waited for: 4 -> 0; matrix products, arithmetic and copies ran while one was open for 1% -> 0% of each run, Pallas kernels for 0% -> 0%
where the time goes in v3:
time: 135 us
  Pallas kernels  134 us (99%)
    pallas_call x1, Pallas kernels, block_of(): pl.pallas_call(functools.partial(block_kernel, members, groups, scale, (*...  131 us
    pallas_call x1, Pallas kernels, finish(): pl.pallas_call(finish_kernel, out_shape=(shape(new.shape, BF16), shape(an...  3.35 us

profile of v3, /device:TPU:1, one launch (start us, length us, event | category | flops | bytes accessed | tf_op | source)
XLA Modules:
  0.0 135.2 jit_solution(17504571678651209333)
XLA Ops:
  1.3 130.6 %block.1 = (bf16[512,512]{1,0:T(8,128)(2,1)}, bf16[32,512]{1,0:T(8,128)(2,1)}, f32[512,512]{1,0:T(8,128)}, bf16[512,512]{1,0:T(8,128)(2,1)}, f32[64,1536]{1,0:T(8,128)}, /*index=5*/f32[64,512]{1,0:T(8,128)}) custom-call(s32[1,16384]{1,0:T(1,128)} %refs_0_.1, bf16[512,512]{1,0:T(8,128)(2,1)} %bitcast.12, bf16[64,512]{1,0:T(8,128)(2,1)} %bitcast.16, ...), custom_call_target="tpu_custom_call" | custom-call | tf_op jit(solution)/shard_map/block/pallas_call | solution.py:652
  131.8 3.4 %finish.1 = (bf16[512,512]{1,0:T(8,128)(2,1)}, bf16[32,512]{1,0:T(8,128)(2,1)}, f32[512,512]{1,0:T(8,128)}, f32[64,512]{1,0:T(8,128)}, f32[64,1024]{1,0:T(8,128)...) custom-call(bf16[512,512]{1,0:T(8,128)(2,1)} %get-tuple-element.20.refs_0_, bf16[32,512]{1,0:T(8,128)(2,1)} %get-tuple-element.21.refs_1_, ...), custom_call_target="tpu_custom_call" | custom-call | tf_op jit(solution)/shard_map/finish/pallas_call | solution.py:678

commit v4 on v3

--- a/solution.py
+++ b/solution.py
@@ -10,6 +10,8 @@
 
 MESH = pl.DeviceIdType.MESH
 F32 = jnp.float32
+HALVES = 2
+TURNS = 4
 BF16 = jnp.bfloat16
 ATOM_SCALE = 0.25
 CAP = 128
@@ -17,7 +19,7 @@
 NEAR_FORWARD = 2
 NEAR_BACKWARD = 4
 SPLIT = 4
-BLOCK_NAMES = 2048
+BLOCK_NAMES = 4096
 BLOCK_FORWARD = 2048
 BLOCK_BACKWARD = 1024
 ANY = pl.BlockSpec(memory_space=pl.ANY)
@@ -88,10 +90,6 @@
     return ref.at[pl.ds(pl.multiple_of(index * rows, rows), rows), :]
 
 
-def some_lanes(ref, index, lanes):
-    return ref.at[:, pl.ds(pl.multiple_of(index * lanes, lanes), lanes)]
-
-
 def tile_of(ref, row, rows, lane, lanes):
     return ref.at[
         pl.ds(pl.multiple_of(row * rows, rows), rows),
@@ -99,8 +97,8 @@
     ]
 
 
-def hot_of_ranks(rank_ref, hot_ref):
-    members, per = rank_ref.shape[:2]
+def hot_of_ranks(rank_ref, hot_ref, first, last):
+    per = rank_ref.shape[1]
     place = lax.broadcasted_iota(jnp.int32, (CAP, LANES), 0).astype(F32)
 
     def one(d):
@@ -111,7 +109,7 @@
                 (place == ranks[q : q + 1, :]).astype(F32).astype(BF16)
             )
 
-    each(0, members, one)
+    each(first, last, one)
 
 
 def block_kernel(members, groups, scale, names_of, *refs):
@@ -215,10 +213,12 @@
 
     def rank_copy(k):
         peer = peer_at(k)
-        return send_to(rank_buf.at[peer], wanted.at[me], all_send.at[0], all_recv.at[0], graph=peer)
+        return send_to(
+            rank_buf.at[peer], wanted.at[members - k], all_send.at[0], all_recv.at[0], graph=peer
+        )
 
     each(1, members, lambda k: rank_copy(k).start(), True)
-    wanted[me] = rank_buf[me]
+    wanted[0] = rank_buf[me]
 
     def look(i):
         high, low = parts_of(i)
@@ -230,8 +230,6 @@
     looks = slots // nblock
     each(0, looks // 2, look)
     drain(wanted.at[0 : members - 1], all_recv.at[0])
-    hot_of_ranks(wanted, hots)
-    chosen[...] = dot(feat, hots[...], NT).astype(BF16)
 
     def feature_tile(index):
         return tile_of(
@@ -239,20 +237,38 @@
         )
 
     def feature_copy(k):
-        peer = peer_at(k)
         return send_to(
-            some_lanes(chosen, peer, CAP), feature_tile(me), all_send.at[1], all_recv.at[1], graph=peer
-        )
-
-    each(1, members, lambda k: feature_copy(k).start(), True)
-    feature_tile(me)[...] = some_lanes(chosen, me, CAP)[...]
+            chosen.at[:, k * CAP : (k + 1) * CAP],
+            feature_tile(me),
+            all_send.at[1],
+            all_recv.at[1],
+            graph=peer_at(k),
+        )
+
+    some = members // TURNS
+    for turn in range(TURNS):
+        hot_of_ranks(wanted, hots, turn * some, (turn + 1) * some)
+        lines = slice(turn * some * CAP, (turn + 1) * some * CAP)
+        chosen[:, lines] = dot(feat, hots[lines, :], NT).astype(BF16)
+        each(max(turn * some, 1), (turn + 1) * some, lambda k: feature_copy(k).start(), True)
+    feature_tile(me)[...] = chosen[:, 0:CAP]
     each(looks // 2, looks, look)
     r["wbil"][...] = wbt_ref[...].astype(F32).T.astype(BF16)
+    target = target_ref[...]
+    atom_dev = atom_ref.shape[0]
+    holder = lax.shift_right_logical(target, atom_dev.bit_length() - 1)
+    line = lax.bitwise_and(holder, 1) * chips + lax.shift_right_logical(holder, 1)
+    line = line * atom_dev + lax.bitwise_and(target, atom_dev - 1)
+    line_hot, line_turn = r["line_hot"], r["line_turn"]
+    lined = (rows_of((line_hot.shape[0], edges)) == line).astype(F32)
+    line_hot[...] = lined.astype(BF16)
+    line_turn[...] = lined.T.astype(BF16)
     drain(chosen.at[:, 0 : (members - 1) * CAP], all_recv.at[1])
     loads[0].wait()
     loads[1].wait()
 
-    outgoing, basis_ref, spread, total_ref = r["outgoing"], r["basis"], r["spread"], r["total"]
+    outgoing, basis_ref, total_ref = r["outgoing"], r["basis"], r["total"]
+    spread = r["spread"]
     fblock = math.gcd(slots, BLOCK_FORWARD)
     far_shift = (NEAR_FORWARD * CAP).bit_length() - 1
     far = members // NEAR_FORWARD
@@ -280,18 +296,19 @@
     parts, half, pair, arrived, grads, slope, gnew = (
         r["parts"], r["half"], r["pair"], r["arrived"], r["grads"], r["slope"], r["gnew"]
     )
-    new_ref, anew_ref = r["new_out"], r["anew_out"]
-    atom_dev = atom_ref.shape[0]
+    new_ref, anew_ref = r["new"], r["anew"]
+
+    def leave(i):
+        key = ("new", "anew", "gin", "wa_all", "wb_all", "wd_all")[i]
+        return pltpu.make_async_copy(r[key], r[key + "_hbm"], load.at[4 + i])
+
     total = total_ref[...]
     high = total.astype(BF16)
     low = (total - high.astype(F32)).astype(BF16)
-    gathered = (dot(wbt_ref[...], high) + dot(wbt_ref[...], low)).astype(BF16)
-    target = target_ref[...]
-    holder = lax.shift_right_logical(target, atom_dev.bit_length() - 1)
-    line = lax.bitwise_and(holder, 1) * chips + lax.shift_right_logical(holder, 1)
-    line = line * atom_dev + lax.bitwise_and(target, atom_dev - 1)
-    line_hot = hot(line, parts.shape[0])
-    part = wide // SPLIT
+    gathered32 = dot(wbt_ref[...], high) + dot(wbt_ref[...], low)
+    gathered = gathered32.astype(BF16)
+    gathered_rows = gathered32.T.astype(BF16)
+    part = wide // HALVES
 
     def pair_copy(q):
         rows = parts.shape[0] // 2
@@ -304,28 +321,32 @@
             graph=partner,
         )
 
-    for q in range(SPLIT):
+    for q in range(HALVES):
         lanes = slice(q * part, (q + 1) * part)
-        update = dot(gathered, wup_ref[:, lanes], TN)
+        update = dot(gathered_rows, wup_ref[:, lanes])
         new = (emb_ref[:, lanes].astype(F32) + silu(update)).astype(BF16)
         new_ref[:, lanes] = new
         slope[:, lanes] = silu_slope(update)
-        parts[:, lanes] = dot(line_hot, new).astype(BF16)
+        parts[:, lanes] = dot(line_hot[...], new).astype(BF16)
         pair_copy(q).start()
 
-    def chip_copy(k):
+    def chip_copy(k, lanes):
         c = chip_at(k)
         return send_to(
-            some_rows(pair, c, atom_dev), arrived.at[chip], all_send.at[3], all_recv.at[3], graph=2 * c + core
-        )
-
-    for q in range(SPLIT):
+            some_rows(pair, c, atom_dev).at[:, lanes],
+            arrived.at[chip, :, lanes],
+            all_send.at[3],
+            all_recv.at[3],
+            graph=2 * c + core,
+        )
+
+    for q in range(HALVES):
         lanes = slice(q * part, (q + 1) * part)
         rows = parts.shape[0] // 2
         own = parts[pl.ds(pl.multiple_of(core * rows, rows), rows), lanes].astype(F32)
         pair_copy(q).wait_recv()
         pair[:, lanes] = (own + half[:, lanes].astype(F32)).astype(BF16)
-    each(1, chips, lambda k: chip_copy(k).start(), True)
+        each(1, chips, lambda k: chip_copy(k, lanes).start(), True)
     arrived[chip] = some_rows(pair, chip, atom_dev)[...]
     loads[2].wait()
     loads[3].wait()
@@ -356,20 +377,22 @@
     wa, wb = r["wa"], r["wb"]
     anew_ref[...] = (atom_ref[...].astype(F32) + silu(pre)).astype(BF16)
     wa[...] = (ATOM_SCALE * dot(asum, grad_pre, TN)).astype(BF16)
+    leave(0).start()
+    leave(1).start()
     each(1, chips, grad_forward, True)
     drain(half, all_recv.at[5])
 
-    picked = dot(hot(line, grads.shape[0]), grads[...], TN)
+    picked = dot(line_turn[...], grads[...])
     grad_new = gedge_ref[...].astype(F32) + picked
     gnew[...] = grad_new
     grad_update = (grad_new * slope[...]).astype(BF16)
     bil_wide = wbt_ref.shape[1]
     wb[:, bil_wide:] = dot(gathered, grad_update)
     gg = dot(wup_ref[...], grad_update, NT).astype(BF16)
-    wb[:, :bil_wide] = dot(gg, high, NT) + dot(gg, low, NT)
-
-    wa_half, wa_pair, wa_in, wa_dp, wa_all = r["wa_half"], r["wa_pair"], r["wa_in"], r["wa_dp"], r["wa_out"]
-    wb_half, wb_pair, wb_in, wb_dp, wb_all = r["wb_half"], r["wb_pair"], r["wb_in"], r["wb_dp"], r["wb_out"]
+    wb[:, :bil_wide] = dot(gg, total_ref[...].astype(BF16), NT)
+
+    wa_half, wa_pair, wa_in, wa_dp, wa_all = r["wa_half"], r["wa_pair"], r["wa_in"], r["wa_dp"], r["wa_all"]
+    wb_half, wb_pair, wb_in, wb_dp, wb_all = r["wb_half"], r["wb_pair"], r["wb_in"], r["wb_dp"], r["wb_all"]
     wa_rows = wa.shape[0] // members
     wb_rows = wb.shape[0] // 8
     wb_lanes = wb.shape[1] // SPLIT
@@ -471,31 +494,37 @@
 
     wa_duo().start()
     wb_duo().start()
+    gg_two = r["gg_two"]
+    gg_two[0:width, :] = gg[:, 0 : edges // 2]
+    gg_two[width:, :] = gg[:, edges // 2 :]
 
     sent, back = r["sent"], r["back"]
-    named, masked, wbil = r["named"], r["masked"], r["wbil"]
+    named, wbil = r["named"], r["wbil"]
     block = math.gcd(slots, BLOCK_BACKWARD)
     blocks = slots // block
     back_far = members // NEAR_BACKWARD
     back_shift = (NEAR_BACKWARD * CAP).bit_length() - 1
     named[...] = jnp.zeros_like(named)
-    acts = {1: sums_pair, 2: sums_far, 7: sums_group, 9: sums_back, 14: sums_pass}
+    acts = {1: sums_pair, 2: sums_far, 8: sums_group, 10: sums_back, 14: sums_pass}
+    masked = r["masked"]
 
     def backward(i):
         for at, act in acts.items():
             pl.when(i == at * blocks // 16)(act)
         here = window(i, block)
-        taken = dot(gg, hot(place_of(i, block), edges)).astype(BF16)
+        place = place_of(i, block)
+        both = dot(gg_two[...], hot(lax.bitwise_and(place, edges // 2 - 1), edges // 2))
+        first = lax.shift_right_arithmetic(place, edges.bit_length() - 2)
+        taken = jnp.where(first == 0, both[0:width], jnp.where(first == 1, both[width:], 0.0)).astype(BF16)
         backed = dot(wbil[...], taken)
         basis = basis_ref[:, here].astype(F32)
         grad = basis[0:1, :] * backed[0:width]
         for b in range(1, basis.shape[0]):
             grad = grad + basis[b : b + 1, :] * backed[b * width : (b + 1) * width]
-        index = name[:, here]
-        source = lax.shift_right_logical(index, back_shift)
+        source = lax.shift_right_logical(name[:, here], back_shift)
         for k in range(back_far):
             masked[k * width : (k + 1) * width, :] = jnp.where(source == k, grad, 0.0).astype(BF16)
-        near = lax.bitwise_and(index, NEAR_BACKWARD * CAP - 1)
+        near = lax.bitwise_and(name[:, window(i, block)], NEAR_BACKWARD * CAP - 1)
         named[...] += dot(masked[...], hot(near, NEAR_BACKWARD * CAP), NT)
 
     each(0, blocks, backward)
@@ -507,19 +536,26 @@
 
     def back_copy(k):
         peer = peer_at(k)
+        there = members - k
         return send_to(
-            sent_tile(peer), some_lanes(back, me, CAP), all_send.at[14], all_recv.at[14], graph=peer
+            sent_tile(peer),
+            back.at[:, there * CAP : (there + 1) * CAP],
+            all_send.at[14],
+            all_recv.at[14],
+            graph=peer,
         )
 
     each(1, members, lambda k: back_copy(k).start(), True)
-    some_lanes(back, me, CAP)[...] = sent_tile(me)[...]
+    back[:, 0:CAP] = sent_tile(me)[...]
     wa_pass().wait_recv()
     wb_pass().wait_recv()
+    leave(3).start()
+    leave(4).start()
     drain(back.at[:, 0 : (members - 1) * CAP], all_recv.at[14])
     grad = dot(back[...], hots[...])
     grad = (grad * r["down_slope"][...]).astype(BF16)
 
-    wd, wd_in, wd_dp, wd_all = r["wd"], r["wd_in"], r["wd_dp"], r["wd_out"]
+    wd, wd_in, wd_dp, wd_all = r["wd"], r["wd_in"], r["wd_dp"], r["wd_all"]
     wd[...] = dot(grad, emb_ref[...])
 
     def wd_tile(ref, index):
@@ -538,7 +574,8 @@
 
     each(1, members, lambda k: wd_far(k).start(), True)
     wd_in[me] = wd_tile(wd, me)[...]
-    r["gin_out"][...] = gnew[...] + dot(grad, wdt_ref[...], TN)
+    r["gin"][...] = gnew[...] + dot(grad, wdt_ref[...], TN)
+    leave(2).start()
     drain(wd_in.at[0 : members - 1], all_recv.at[15])
     wd_dp[group] = jnp.sum(wd_in[...], axis=0)
     each(1, groups, lambda k: wd_group(k).start(), True)
@@ -567,6 +604,9 @@
     drain(wd_in.at[0 : members - 1], all_send.at[15])
     drain(wd_in.at[0 : members - 1], all_send.at[16])
     drain(wd_in.at[0 : members - 1], all_recv.at[16])
+    leave(5).start()
+    for i in range(6):
+        leave(i).wait()
 
 
 def block_of(values, members, groups, scale):
@@ -597,14 +637,15 @@
             specs.append(pl.BlockSpec(memory_space=pltpu.SMEM) if key == "count" else VMEM)
         args.append(value)
     outs = {
-        "new_out": shape((edges, wide), BF16),
-        "anew_out": shape((atom_dev, wide), BF16),
-        "gin_out": shape((edges, wide), F32),
-        "wa_out": shape((wide, wide), BF16),
-        "wb_out": shape((width, all_wide), F32),
-        "wd_out": shape((width, wide), F32),
+        "new": shape((edges, wide), BF16),
+        "anew": shape((atom_dev, wide), BF16),
+        "gin": shape((edges, wide), F32),
+        "wa_all": shape((wide, wide), BF16),
+        "wb_all": shape((width, all_wide), F32),
+        "wd_all": shape((width, wide), F32),
     }
     scratch = {key: pltpu.VMEM(values[key].shape, values[key].dtype) for key in late}
+    scratch |= {key: pltpu.VMEM(out.shape, out.dtype) for key, out in outs.items()}
     scratch |= {
         "table": pltpu.VMEM((highs, LANES), BF16),
         "found": pltpu.VMEM((highs, LANES), F32),
@@ -618,6 +659,8 @@
         "wbil": pltpu.VMEM((rows, width), BF16),
         "spread": pltpu.VMEM((rows, math.gcd(slots, BLOCK_FORWARD)), BF16),
         "total": pltpu.VMEM((rows, edges), F32),
+        "line_hot": pltpu.VMEM((atoms, edges), BF16),
+        "line_turn": pltpu.VMEM((edges, atoms), BF16),
         "parts": pltpu.VMEM((atoms, wide), BF16),
         "half": pltpu.VMEM((atoms // 2, wide), BF16),
         "pair": pltpu.VMEM((atoms // 2, wide), BF16),
@@ -635,6 +678,7 @@
         "wb_pair": pltpu.VMEM((width // 2, all_wide), F32),
         "wb_in": pltpu.VMEM((chips, *piece), F32),
         "wb_dp": pltpu.VMEM((groups, *piece), F32),
+        "gg_two": pltpu.VMEM((2 * width, edges // 2), BF16),
         "named": pltpu.VMEM((back_far * width, NEAR_BACKWARD * CAP), F32),
         "masked": pltpu.VMEM((back_far * width, math.gcd(slots, BLOCK_BACKWARD)), BF16),
         "sent": pltpu.VMEM((back_far * width, NEAR_BACKWARD * CAP), BF16),
@@ -647,13 +691,13 @@
         "many_recv": pltpu.SemaphoreType.DMA((2, chips)),
         "dp_send": pltpu.SemaphoreType.DMA((3,)),
         "dp_recv": pltpu.SemaphoreType.DMA((3,)),
-        "load": pltpu.SemaphoreType.DMA((4,)),
+        "load": pltpu.SemaphoreType.DMA((10,)),
     }
     return pl.pallas_call(
-        functools.partial(block_kernel, members, groups, scale, (*ins, *outs, *scratch)),
+        functools.partial(block_kernel, members, groups, scale, (*ins, *(key + "_hbm" for key in outs), *scratch)),
         out_shape=tuple(outs.values()),
         in_specs=specs,
-        out_specs=(VMEM,) * len(outs),
+        out_specs=(ANY,) * len(outs),
         scratch_shapes=list(scratch.values()),
         compiler_params=params(collective_id=1, has_side_effects=True),
         name="block",
@@ -661,20 +705,39 @@
 
 
 def finish_kernel(*refs):
-    new, anew, gin, wa, wb, wd, new_o, anew_o, gin_o, down_o, bil_o, up_o, gat_o = refs
-    new_o[...] = new[...]
-    anew_o[...] = anew[...]
-    gin_o[...] = gin[...]
-    down_o[...] = wd[...]
-    bil_o[...] = wb[:, : bil_o.shape[1]]
-    up_o[...] = wb[:, bil_o.shape[1] :]
-    gat_o[...] = wa[...].astype(F32)
+    ins, outs, bufs, (wide_buf, got, put) = refs[:6], refs[6:13], refs[13:19], refs[19:]
+    new, anew, gin, wa, wb, wd = bufs
+    takes = [pltpu.make_async_copy(ins[i], bufs[i], got.at[i]) for i in range(6)]
+    order = (3, 2, 0, 4, 5, 1)
+    for i in order:
+        takes[i].start()
+    bil_wide = outs[4].shape[1]
+    gives = {
+        3: [(wide_buf, outs[6])],
+        2: [(gin, outs[2])],
+        0: [(new, outs[0])],
+        4: [(wb.at[:, 0:bil_wide], outs[4]), (wb.at[:, bil_wide:], outs[5])],
+        5: [(wd, outs[3])],
+        1: [(anew, outs[1])],
+    }
+    started = []
+    for i in order:
+        takes[i].wait()
+        if i == 3:
+            wide_buf[...] = wa[...].astype(F32)
+        for src, dst in gives[i]:
+            one = pltpu.make_async_copy(src, dst, put.at[len(started)])
+            one.start()
+            started.append(one)
+    for one in started:
+        one.wait()
 
 
 def finish(new, anew, gin, wa, wb, wd):
     shape = jax.ShapeDtypeStruct
     wide = wa.shape[1]
     width = wb.shape[0]
+    ins = (new, anew, gin, wa, wb, wd)
     return pl.pallas_call(
         finish_kernel,
         out_shape=(
@@ -686,11 +749,13 @@
             shape((width, wide), F32),
             shape(wa.shape, F32),
         ),
-        in_specs=[VMEM] * 6,
-        out_specs=(VMEM,) * 7,
+        in_specs=[ANY] * 6,
+        out_specs=(ANY,) * 7,
+        scratch_shapes=[pltpu.VMEM(one.shape, one.dtype) for one in ins]
+        + [pltpu.VMEM(wa.shape, F32), pltpu.SemaphoreType.DMA((6,)), pltpu.SemaphoreType.DMA((7,))],
         compiler_params=params(),
         name="finish",
-    )(new, anew, gin, wa, wb, wd)
+    )(*ins)
 
 
 def body(

time: 135 us -> 130 us (0.963)
  Pallas kernels: 134 us -> 129 us
    pallas_call x1, Pallas kernels: 131 us -> 126 us  [block_of(): pl.pallas_call(functools.partial(block_kernel, members, groups, scale, (*...]
where the time goes in v4:
time: 130 us
  Pallas kernels  129 us (99%)
    pallas_call x1, Pallas kernels, block_of(): pl.pallas_call(functools.partial(block_kernel, members, groups, scale, (*...  126 us
    pallas_call x1, Pallas kernels, finish(): pl.pallas_call(finish_kernel, out_shape=(shape(new.shape, BF16), shape(an...  2.88 us

profile of v4, /device:TPU:1, one launch (start us, length us, event | category | flops | bytes accessed | tf_op | source)
XLA Modules:
  0.0 129.9 jit_solution(13738546877995451523)
XLA Ops:
  1.3 125.7 %block.1 = (bf16[512,512]{1,0:T(8,128)(2,1)}, bf16[32,512]{1,0:T(8,128)(2,1)}, f32[512,512]{1,0:T(8,128)}, bf16[512,512]{1,0:T(8,128)(2,1)}, f32[64,1536]{1,0:T(8,128)}, /*index=5*/f32[64,512]{1,0:T(8,128)}) custom-call(s32[1,16384]{1,0:T(1,128)} %refs_0_.1, bf16[512,512]{1,0:T(8,128)(2,1)} %bitcast.12, bf16[64,512]{1,0:T(8,128)(2,1)} %bitcast.16, ...), custom_call_target="tpu_custom_call" | custom-call | tf_op jit(solution)/shard_map/block/pallas_call | solution.py:696
  127.0 2.9 %finish.1 = (bf16[512,512]{1,0:T(8,128)(2,1)}, bf16[32,512]{1,0:T(8,128)(2,1)}, f32[512,512]{1,0:T(8,128)}, f32[64,512]{1,0:T(8,128)}, f32[64,1024]{1,0:T(8,128)...) custom-call(bf16[512,512]{1,0:T(8,128)(2,1)} %get-tuple-element.20.refs_0_, bf16[32,512]{1,0:T(8,128)(2,1)} %get-tuple-element.21.refs_1_, ...), custom_call_target="tpu_custom_call" | custom-call | tf_op jit(solution)/shard_map/finish/pallas_call | solution.py:741

commit v5 on v4

--- a/solution.py
+++ b/solution.py
@@ -21,7 +21,7 @@
 SPLIT = 4
 BLOCK_NAMES = 4096
 BLOCK_FORWARD = 2048
-BLOCK_BACKWARD = 1024
+BLOCK_BACKWARD = 2048
 ANY = pl.BlockSpec(memory_space=pl.ANY)
 VMEM = pl.BlockSpec(memory_space=pltpu.VMEM)
 NN = (((1,), (0,)), ((), ()))
@@ -326,7 +326,7 @@
         update = dot(gathered_rows, wup_ref[:, lanes])
         new = (emb_ref[:, lanes].astype(F32) + silu(update)).astype(BF16)
         new_ref[:, lanes] = new
-        slope[:, lanes] = silu_slope(update)
+        slope[:, lanes] = update
         parts[:, lanes] = dot(line_hot[...], new).astype(BF16)
         pair_copy(q).start()
 
@@ -348,6 +348,7 @@
         pair[:, lanes] = (own + half[:, lanes].astype(F32)).astype(BF16)
         each(1, chips, lambda k: chip_copy(k, lanes).start(), True)
     arrived[chip] = some_rows(pair, chip, atom_dev)[...]
+    slope[...] = silu_slope(slope[...])
     loads[2].wait()
     loads[3].wait()
     watom_ref, gedge_ref = r["watom"], r["gedge"]
@@ -377,9 +378,15 @@
     wa, wb = r["wa"], r["wb"]
     anew_ref[...] = (atom_ref[...].astype(F32) + silu(pre)).astype(BF16)
     wa[...] = (ATOM_SCALE * dot(asum, grad_pre, TN)).astype(BF16)
+    def wa_duo():
+        return send_to(
+            some_rows(wa, other, wa.shape[0] // 2), r["wa_half"], all_send.at[6], all_recv.at[6], graph=partner
+        )
+
     leave(0).start()
     leave(1).start()
     each(1, chips, grad_forward, True)
+    wa_duo().start()
     drain(half, all_recv.at[5])
 
     picked = dot(line_turn[...], grads[...])
@@ -401,11 +408,6 @@
     def wb_tile(ref, c, base):
         return tile_of(ref, base * wb_split + lax.div(c, SPLIT), wb_rows, lax.rem(c, SPLIT), wb_lanes)
 
-    def wa_duo():
-        return send_to(
-            some_rows(wa, other, wa.shape[0] // 2), wa_half, all_send.at[6], all_recv.at[6], graph=partner
-        )
-
     def wb_duo():
         return send_to(
             some_rows(wb, other, wb.shape[0] // 2), wb_half, all_send.at[7], all_recv.at[7], graph=partner
@@ -492,7 +494,6 @@
         wa_pass().start()
         wb_pass().start()
 
-    wa_duo().start()
     wb_duo().start()
     gg_two = r["gg_two"]
     gg_two[0:width, :] = gg[:, 0 : edges // 2]
@@ -505,7 +506,7 @@
     back_far = members // NEAR_BACKWARD
     back_shift = (NEAR_BACKWARD * CAP).bit_length() - 1
     named[...] = jnp.zeros_like(named)
-    acts = {1: sums_pair, 2: sums_far, 8: sums_group, 10: sums_back, 14: sums_pass}
+    acts = {1: sums_pair, 2: sums_far, 9: sums_group, 11: sums_back}
     masked = r["masked"]
 
     def backward(i):
@@ -547,6 +548,7 @@
 
     each(1, members, lambda k: back_copy(k).start(), True)
     back[:, 0:CAP] = sent_tile(me)[...]
+    sums_pass()
     wa_pass().wait_recv()
     wb_pass().wait_recv()
     leave(3).start()

time: 130 us -> 126 us (0.969)
  Pallas kernels: 129 us -> 125 us
    pallas_call x1, Pallas kernels: 126 us -> 122 us  [block_of(): pl.pallas_call(functools.partial(block_kernel, members, groups, scale, (*...]
where the time goes in v5:
time: 126 us
  Pallas kernels  125 us (99%)
  between operations  1.45 us (1%)
    pallas_call x1, Pallas kernels, block_of(): pl.pallas_call(functools.partial(block_kernel, members, groups, scale, (*...  122 us
    pallas_call x1, Pallas kernels, finish(): pl.pallas_call(finish_kernel, out_shape=(shape(new.shape, BF16), shape(an...  2.88 us

profile of v5, /device:TPU:1, one launch (start us, length us, event | category | flops | bytes accessed | tf_op | source)
XLA Modules:
  0.0 126.0 jit_solution(13089550081328598142)
XLA Ops:
  1.3 121.7 %block.1 = (bf16[512,512]{1,0:T(8,128)(2,1)}, bf16[32,512]{1,0:T(8,128)(2,1)}, f32[512,512]{1,0:T(8,128)}, bf16[512,512]{1,0:T(8,128)(2,1)}, f32[64,1536]{1,0:T(8,128)}, /*index=5*/f32[64,512]{1,0:T(8,128)}) custom-call(s32[1,16384]{1,0:T(1,128)} %refs_0_.1, bf16[512,512]{1,0:T(8,128)(2,1)} %bitcast.12, bf16[64,512]{1,0:T(8,128)(2,1)} %bitcast.16, ...), custom_call_target="tpu_custom_call" | custom-call | tf_op jit(solution)/shard_map/block/pallas_call | solution.py:698
  123.0 2.9 %finish.1 = (bf16[512,512]{1,0:T(8,128)(2,1)}, bf16[32,512]{1,0:T(8,128)(2,1)}, f32[512,512]{1,0:T(8,128)}, f32[64,512]{1,0:T(8,128)}, f32[64,1024]{1,0:T(8,128)...) custom-call(bf16[512,512]{1,0:T(8,128)(2,1)} %get-tuple-element.20.refs_0_, bf16[32,512]{1,0:T(8,128)(2,1)} %get-tuple-element.21.refs_1_, ...), custom_call_target="tpu_custom_call" | custom-call | tf_op jit(solution)/shard_map/finish/pallas_call | solution.py:743

commit v6 on v5

--- a/solution.py
+++ b/solution.py
@@ -20,7 +20,7 @@
 NEAR_BACKWARD = 4
 SPLIT = 4
 BLOCK_NAMES = 4096
-BLOCK_FORWARD = 2048
+BLOCK_FORWARD = 4096
 BLOCK_BACKWARD = 2048
 ANY = pl.BlockSpec(memory_space=pl.ANY)
 VMEM = pl.BlockSpec(memory_space=pltpu.VMEM)

time: 126 us -> 126 us (level)
  no operation moved by 1% of the time
where the time goes in v6:
time: 126 us; the launch traced here: 125 us
  Pallas kernels  124 us (98%)
  between operations  1.45 us (1%)
    pallas_call x1, Pallas kernels, block_of(): pl.pallas_call(functools.partial(block_kernel, members, groups, scale, (*...  121 us
    pallas_call x1, Pallas kernels, finish(): pl.pallas_call(finish_kernel, out_shape=(shape(new.shape, BF16), shape(an...  2.88 us

profile of v6, /device:TPU:1, one launch (start us, length us, event | category | flops | bytes accessed | tf_op | source)
XLA Modules:
  0.0 125.4 jit_solution(10224248689668633613)
XLA Ops:
  1.3 121.1 %block.1 = (bf16[512,512]{1,0:T(8,128)(2,1)}, bf16[32,512]{1,0:T(8,128)(2,1)}, f32[512,512]{1,0:T(8,128)}, bf16[512,512]{1,0:T(8,128)(2,1)}, f32[64,1536]{1,0:T(8,128)}, /*index=5*/f32[64,512]{1,0:T(8,128)}) custom-call(s32[1,16384]{1,0:T(1,128)} %refs_0_.1, bf16[512,512]{1,0:T(8,128)(2,1)} %bitcast.12, bf16[64,512]{1,0:T(8,128)(2,1)} %bitcast.16, ...), custom_call_target="tpu_custom_call" | custom-call | tf_op jit(solution)/shard_map/block/pallas_call | solution.py:698
  122.4 2.9 %finish.1 = (bf16[512,512]{1,0:T(8,128)(2,1)}, bf16[32,512]{1,0:T(8,128)(2,1)}, f32[512,512]{1,0:T(8,128)}, f32[64,512]{1,0:T(8,128)}, f32[64,1024]{1,0:T(8,128)...) custom-call(bf16[512,512]{1,0:T(8,128)(2,1)} %get-tuple-element.20.refs_0_, bf16[32,512]{1,0:T(8,128)(2,1)} %get-tuple-element.21.refs_1_, ...), custom_call_target="tpu_custom_call" | custom-call | tf_op jit(solution)/shard_map/finish/pallas_call | solution.py:743
